TPU v7x, 512 devices: a whole 4x4x16 slice. The times are simulated.
512 devices in a mesh: ctx: 32 (over y, x, z_hi), head: 16 (over z_lo, core).
Axes of the slice: x: 4, y: 4, z: 16 (z_hi: 2, z_lo: 8; z = z_hi * 8 + z_lo), core: 2. Of those that a mesh axis runs over, the one named last changes fastest.
Arguments:
- tokens: bfloat16 [14336, 5376], P('ctx'), may hold values from -6 to 6
- w_query: bfloat16 [5376, 4096], P('ctx', 'head')
- key_weight: bfloat16 [5376, 2048], P('ctx', 'head')
- value_weight: bfloat16 [5376, 2048], P('ctx', 'head'), may hold values from -0.078125 to 0.078125
- query_gain: float32 [128], replicated, may hold values from 0.5 to 16
- key_gain: float32 [128], replicated, may hold values from 0.5 to 16
Outputs:
- attended: bfloat16 [14336, 4096], P('ctx', 'head')
All inputs are finite; a program needn't handle non-finite values.
Results may differ from a plain program's by a relative error of at most 0.025.
Values may be sent and summed in bfloat16 or wider, within the bound.
No kernel may reach another device: no remote copies, remote signals or barrier semaphores. Data moves between devices by JAX's collectives and lax.ppermute only.
A program may use at most 64 MiB of HBM per device.

v0:
```python
import jax
import jax.numpy as jnp
from jax import lax
from jax.sharding import PartitionSpec as P

WINDOW = 1024


query_scale = 168.0 ** (-0.5)


def from_behind(block, axis, distance):
    devices = range(lax.axis_size(axis))
    route = [(i - distance, i) for i in devices if i - distance in devices]
    return lax.ppermute(block, axis, route)


def normalize(values, gain):
    return values * lax.rsqrt(jnp.mean(values * values, axis=-1, keepdims=True) + 1e-06) * gain


def rotate(values, position):
    half = values.shape[-1] // 2
    expo = jnp.arange(half, dtype=jnp.float32) * (2.0 / values.shape[-1])
    freq = jnp.power(jnp.float32(10000.0), -expo)
    angle = position[:, None] * freq[None, :]
    cosine = jnp.cos(angle)[:, None, :]
    sine = jnp.sin(angle)[:, None, :]
    first = values[..., :half]
    second = values[..., half:]
    return jnp.concatenate(
        [first * cosine - second * sine, second * cosine + first * sine], axis=-1
    )


def fold_rows(tokens, piece):
    return jnp.dot(tokens, piece, preferred_element_type=jnp.float32)


def on_device(tokens, w_query, key_weight, value_weight, query_gain, key_gain):
    row_count = tokens.shape[0]
    head_size = query_gain.shape[0]
    kv_local = key_weight.shape[1] // head_size
    q_width = w_query.shape[1]

    def add_one(piece):
        return fold_rows(tokens, piece)

    query_sum = add_one(lax.all_gather(w_query, "ctx", axis=0, tiled=True))
    summed_keys = add_one(lax.all_gather(key_weight, "ctx", axis=0, tiled=True))
    summed_values = add_one(lax.all_gather(value_weight, "ctx", axis=0, tiled=True))
    offset = lax.axis_index("ctx") * row_count
    local_pos = offset + jnp.arange(row_count, dtype=jnp.int32)
    position = local_pos.astype(jnp.float32)
    queries = rotate(
        normalize(query_sum.reshape(row_count, 2 * kv_local, head_size), query_gain), position
    ).astype(jnp.bfloat16)
    keys = rotate(
        normalize(summed_keys.reshape(row_count, kv_local, head_size), key_gain), position
    ).astype(jnp.bfloat16)
    values = summed_values.reshape(row_count, kv_local, head_size).astype(jnp.bfloat16)
    reach = WINDOW - 1
    hop_count = (reach + row_count - 1) // row_count
    needed = [min(row_count, reach - distance * row_count) for distance in range(hop_count)]
    received = []
    carried = (keys, values)
    for distance in range(hop_count):
        arrived = from_behind((carried[0], carried[1]), "ctx", 1)
        received.append(arrived)
        if distance + 1 < hop_count:
            keep = needed[distance + 1]
            cut = needed[distance] - keep
            carried = (arrived[0][cut:], arrived[1][cut:])
    all_keys = jnp.concatenate([piece[0] for piece in reversed(received)] + [keys], axis=0)
    all_values = jnp.concatenate([piece[1] for piece in reversed(received)] + [values], axis=0)
    key_pos = offset - reach + jnp.arange(reach + row_count, dtype=jnp.int32)
    allowed = (
        (key_pos[None, :] <= local_pos[:, None])
        & (key_pos[None, :] > local_pos[:, None] - WINDOW)
        & (key_pos[None, :] >= 0)
    )
    grouped_heads = queries.reshape(row_count, kv_local, 2, head_size)
    scores = (
        jnp.einsum("bkgd,ckd->kgbc", grouped_heads, all_keys, preferred_element_type=jnp.float32)
        * query_scale
    )
    scores = jnp.where(allowed[None, None], scores, jnp.float32(-1e30))
    top = jnp.max(scores, axis=-1, keepdims=True)
    weights = jnp.exp(scores - top)
    probs = (weights / jnp.sum(weights, axis=-1, keepdims=True)).astype(jnp.bfloat16)
    mixed = jnp.einsum("kgbc,ckd->bkgd", probs, all_values, preferred_element_type=jnp.float32)
    return mixed.reshape(row_count, q_width).astype(jnp.bfloat16)


def solution(mesh):
    placed = (P("ctx", None), P("ctx", "head"), P("ctx", "head"), P("ctx", "head"), P(), P())
    return jax.shard_map(
        on_device, mesh=mesh, in_specs=placed, out_specs=P("ctx", "head"), check_vma=False
    )
```

profile of v0, /device:TPU:2, one launch (start us, length us, event | category | flops | bytes accessed | tf_op | source)
XLA Modules:
  0.0 406.5 jit_solution(15615109111452498067)
XLA Ops:
  6.5 0.0 copy-start.1
  6.5 0.0 all-gather.6.cloned.1.call-start
  6.5 0.7 all-gather.6.cloned.1.call-update
  7.3 0.0 all-gather.4.cloned.1.call-start
  7.3 0.7 all-gather.4.cloned.1.call-update
  8.0 0.0 all-gather.8.cloned.1.call-start
  8.1 0.7 all-gather.8.cloned.1.call-update
  8.8 123.6 %all-gather.6.cloned.1.call-done = bf16[5376,128]{1,0:T(8,128)(2,1)} async-done(((bf16[168,128]{1,0:T(8,128)(2,1)}), bf16[5376,128]{1,0:T(8,128)(2,1)}) %all-gather.6.cloned.1.call-update) | async-done | bytes 1376272 | tf_op jit(solution)/shard_map/all_gather | solution.py:50
  132.3 4.3 %multiply_reduce_fusion.1 = (f32[448]{0:T(512)S(1)}, f32[448,128]{1,0:T(8,128)S(1)}) fusion(bf16[448,5376]{1,0:T(8,128)(2,1)} %param.6, bf16[5376,128]{1,0:T(8,128)(2,1)} %all-gather.6.cloned.1.call-done), kind=kOutput, calls=%fused_computation.35 | convolution fusion | flops 616676928 | bytes 6424320 | tf_op jit(solution)/shard_map/dot_general | solution.py:37
  136.6 0.0 copy-done.1
  136.7 0.1 multiply_bitcast_fusion
  136.8 1.1 fusion.18
  137.9 0.1 pad_maximum_fusion
  138.0 1.9 collective-permute-start.3
  139.9 104.3 %all-gather.4.cloned.1.call-done = bf16[5376,128]{1,0:T(8,128)(2,1)} async-done(((bf16[168,128]{1,0:T(8,128)(2,1)}), bf16[5376,128]{1,0:T(8,128)(2,1)}) %all-gather.4.cloned.1.call-update) | async-done | bytes 1376272 | tf_op jit(solution)/shard_map/all_gather | solution.py:51
  244.2 4.2 %fusion.9 = bf16[448,1,128]{2,0,1:T(8,128)(2,1)S(1)} fusion(bf16[448,5376]{1,0:T(8,128)(2,1)} %param.6, bf16[5376,128]{1,0:T(8,128)(2,1)} %all-gather.4.cloned.1.call-done), kind=kOutput, calls=%fused_computation.10 | convolution fusion | flops 616620032 | bytes 6307840 | tf_op jit(solution)/shard_map/dot_general | solution.py:37
  248.4 1.9 collective-permute-start
  250.3 0.0 collective-permute-done.3
  250.4 13.2 %collective-permute-start.4 = (bf16[448,1,128]{2,0,1:T(8,128)(2,1)S(1)}, bf16[448,1,128]{2,0,1:T(8,128)(2,1)S(1)}, u32[]{:S(2)}, u32[]{:S(2)}) collective-permute-start(bf16[448,1,128]{2,0,1:T(8,128)(2,1)S(1)} %collective-permute-done.3), channel_id=1, source_target_pairs={{0,16},{16,32},{32,48},{48,64},{64,80},{80,96},{96,112},{112,128},... | collective-permute-start | bytes 344072 | tf_op jit(solution)/shard_map/ppermute | solution.py:15
  263.6 17.1 %collective-permute-done = bf16[448,1,128]{2,0,1:T(8,128)(2,1)S(1)} collective-permute-done((bf16[448,1,128]{2,0,1:T(8,128)(2,1)S(1)}, bf16[448,1,128]{2,0,1:T(8,128)(2,1)S(1)}, u32[]{:S(2)}, u32[]{:S(2)}) %collective-permute-start) | collective-permute-done | bytes 114720 | tf_op jit(solution)/shard_map/ppermute | solution.py:15
  280.7 1.9 collective-permute-start.1
  282.6 0.7 and_and_fusion
  283.4 5.9 %collective-permute-done.4 = bf16[448,1,128]{2,0,1:T(8,128)(2,1)S(1)} collective-permute-done((bf16[448,1,128]{2,0,1:T(8,128)(2,1)S(1)}, bf16[448,1,128]{2,0,1:T(8,128)(2,1)S(1)}, u32[]{:S(2)}, u32[]{:S(2)}) %collective-permute-start.4) | collective-permute-done | bytes 114720 | tf_op jit(solution)/shard_map/ppermute | solution.py:15
  289.3 7.0 %collective-permute-start.5 = (bf16[127,1,128]{2,0,1:T(8,128)(2,1)S(1)}, bf16[127,1,128]{2,0,1:T(8,128)(2,1)S(1)}, u32[]{:S(2)}, u32[]{:S(2)}) collective-permute-start(bf16[127,1,128]{2,0,1:T(8,128)(2,1)S(1)} %slice.27), channel_id=1, source_target_pairs={{0,16},{16,32},{32,48},{48,64},{64,80},{80,96},{96,112},{112,128},... | collective-permute-start | bytes 97544 | tf_op jit(solution)/shard_map/ppermute | solution.py:15
  296.2 2.6 collective-permute-done.1
  298.8 5.2 %collective-permute-start.2 = (bf16[127,1,128]{2,0,1:T(8,128)(2,1)S(1)}, bf16[127,1,128]{2,0,1:T(8,128)(2,1)S(1)}, u32[]{:S(2)}, u32[]{:S(2)}) collective-permute-start(bf16[127,1,128]{2,0,1:T(8,128)(2,1)S(1)} %slice.24), channel_id=1, source_target_pairs={{0,16},{16,32},{32,48},{48,64},{64,80},{80,96},{96,112},{112,128},... | collective-permute-start | bytes 97544 | tf_op jit(solution)/shard_map/ppermute | solution.py:15
  304.0 0.9 multiply_cosine_fusion
  304.9 0.5 collective-permute-done.5
  305.4 1.6 concatenate.26
  307.0 8.0 %collective-permute-done.2 = bf16[127,1,128]{2,0,1:T(8,128)(2,1)S(1)} collective-permute-done((bf16[127,1,128]{2,0,1:T(8,128)(2,1)S(1)}, bf16[127,1,128]{2,0,1:T(8,128)(2,1)S(1)}, u32[]{:S(2)}, u32[]{:S(2)}) %collective-permute-start.2) | collective-permute-done | bytes 32544 | tf_op jit(solution)/shard_map/ppermute | solution.py:15
  315.0 1.6 concatenate.24
  316.6 0.0 copy-start
  316.6 72.9 %all-gather.8.cloned.1.call-done = bf16[5376,256]{1,0:T(8,128)(2,1)} async-done(((bf16[168,256]{1,0:T(8,128)(2,1)}), bf16[5376,256]{1,0:T(8,128)(2,1)}) %all-gather.8.cloned.1.call-update) | async-done | bytes 2752528 | tf_op jit(solution)/shard_map/all_gather | solution.py:49
  389.5 4.6 %fusion.28 = f32[448,256]{1,0:T(8,128)S(1)} fusion(bf16[448,5376]{1,0:T(8,128)(2,1)} %param.6, bf16[5376,256]{1,0:T(8,128)(2,1)} %all-gather.8.cloned.1.call-done), kind=kOutput, calls=%fused_computation.47 | convolution fusion | flops 1233125376 | bytes 8028160 | tf_op jit(solution)/shard_map/dot_general | solution.py:37
  394.2 0.2 reshape.288
  394.4 0.5 multiply_reduce_fusion
  395.0 0.1 copy.13
  395.1 0.0 copy-done
  395.1 0.2 fusion.10
  395.3 0.2 subtract_convert_fusion
  395.6 1.5 fusion.27
  397.1 0.9 fusion
  398.0 1.0 fusion.6
  399.0 0.2 copy.15
  399.2 0.7 copy.20
  (9 shorter events, 0.1 us)
Async XLA Ops:
  6.5 130.1 %copy-start.1 = (f32[128]{0:T(128)S(1)}, f32[128]{0:T(128)}, u32[]{:S(2)}) copy-start(f32[128]{0:T(128)} %param.11) | copy-start | bytes 1540
  6.5 125.8 %all-gather.6.cloned.1.call-start = ((), (), s32[]{:S(2)}) async-start(), calls=%async_computation.1 | async-start | bytes 1419264 | tf_op jit(solution)/shard_map/all_gather | solution.py:50
  7.3 236.9 %all-gather.4.cloned.1.call-start = ((), (), s32[]{:S(2)}) async-start(), calls=%async_computation | async-start | bytes 1419264 | tf_op jit(solution)/shard_map/all_gather | solution.py:51
  8.0 381.5 %all-gather.8.cloned.1.call-start = ((), (), s32[]{:S(2)}) async-start(), calls=%async_computation.2 | async-start | bytes 2838528 | tf_op jit(solution)/shard_map/all_gather | solution.py:49
  138.0 112.4 %collective-permute-start.3 = (bf16[448,1,128]{2,0,1:T(8,128)(2,1)S(1)}, bf16[448,1,128]{2,0,1:T(8,128)(2,1)S(1)}, u32[]{:S(2)}, u32[]{:S(2)}) collective-permute-start(bf16[448,1,128]{2,0,1:T(8,128)(2,1)S(1)} %pad_maximum_fusion), channel_id=1, source_target_pairs={{0,16},{16,32},{32,48},{48,64},{64,80},{80,96},{96,112},{112,128},... | collective-permute-start | bytes 344072 | tf_op jit(solution)/shard_map/ppermute | solution.py:15
  248.4 32.3 %collective-permute-start = (bf16[448,1,128]{2,0,1:T(8,128)(2,1)S(1)}, bf16[448,1,128]{2,0,1:T(8,128)(2,1)S(1)}, u32[]{:S(2)}, u32[]{:S(2)}) collective-permute-start(bf16[448,1,128]{2,0,1:T(8,128)(2,1)S(1)} %fusion.9), channel_id=1, source_target_pairs={{0,16},{16,32},{32,48},{48,64},{64,80},{80,96},{96,112},{112,128},... | collective-permute-start | bytes 344072 | tf_op jit(solution)/shard_map/ppermute | solution.py:15
  250.4 38.9 %collective-permute-start.4 = (bf16[448,1,128]{2,0,1:T(8,128)(2,1)S(1)}, bf16[448,1,128]{2,0,1:T(8,128)(2,1)S(1)}, u32[]{:S(2)}, u32[]{:S(2)}) collective-permute-start(bf16[448,1,128]{2,0,1:T(8,128)(2,1)S(1)} %collective-permute-done.3), channel_id=1, source_target_pairs={{0,16},{16,32},{32,48},{48,64},{64,80},{80,96},{96,112},{112,128},... | collective-permute-start | bytes 344072 | tf_op jit(solution)/shard_map/ppermute | solution.py:15
  280.7 18.0 %collective-permute-start.1 = (bf16[448,1,128]{2,0,1:T(8,128)(2,1)S(1)}, bf16[448,1,128]{2,0,1:T(8,128)(2,1)S(1)}, u32[]{:S(2)}, u32[]{:S(2)}) collective-permute-start(bf16[448,1,128]{2,0,1:T(8,128)(2,1)S(1)} %collective-permute-done), channel_id=1, source_target_pairs={{0,16},{16,32},{32,48},{48,64},{64,80},{80,96},{96,112},{112,128},... | collective-permute-start | bytes 344072 | tf_op jit(solution)/shard_map/ppermute | solution.py:15
  289.3 16.1 %collective-permute-start.5 = (bf16[127,1,128]{2,0,1:T(8,128)(2,1)S(1)}, bf16[127,1,128]{2,0,1:T(8,128)(2,1)S(1)}, u32[]{:S(2)}, u32[]{:S(2)}) collective-permute-start(bf16[127,1,128]{2,0,1:T(8,128)(2,1)S(1)} %slice.27), channel_id=1, source_target_pairs={{0,16},{16,32},{32,48},{48,64},{64,80},{80,96},{96,112},{112,128},... | collective-permute-start | bytes 97544 | tf_op jit(solution)/shard_map/ppermute | solution.py:15
  298.8 16.2 %collective-permute-start.2 = (bf16[127,1,128]{2,0,1:T(8,128)(2,1)S(1)}, bf16[127,1,128]{2,0,1:T(8,128)(2,1)S(1)}, u32[]{:S(2)}, u32[]{:S(2)}) collective-permute-start(bf16[127,1,128]{2,0,1:T(8,128)(2,1)S(1)} %slice.24), channel_id=1, source_target_pairs={{0,16},{16,32},{32,48},{48,64},{64,80},{80,96},{96,112},{112,128},... | collective-permute-start | bytes 97544 | tf_op jit(solution)/shard_map/ppermute | solution.py:15
  316.6 78.5 %copy-start = (f32[128]{0:T(128)S(1)}, f32[128]{0:T(128)}, u32[]{:S(2)}) copy-start(f32[128]{0:T(128)} %param.10) | copy-start | bytes 1540
Sparse Core Ops, SparseCore 0:
  11.7 120.5 all-gather.5
  136.7 107.4 all-gather.3
  248.6 140.9 all-gather.7
where the time goes:
time: 407 us; the launch traced here: 406 us
  waiting for transfers between devices  337 us (83%)
  starting transfers between devices  31.2 us (8%)
  matrix products  15.6 us (4%)
  between operations  13.3 us (3%)
  other arithmetic  4.81 us (1%)
  local copies, waits for them, and re-layouts  4.53 us (1%)
    all_gather x1, waiting for transfers between devices, on_device(): summed_keys = add_one(lax.all_gather(key_weight, 'ctx', axis=0, tiled=True))  124 us
    all_gather x1, waiting for transfers between devices, on_device(): lax.all_gather(value_weight, 'ctx', axis=0, tiled=True)  104 us
    all_gather x1, waiting for transfers between devices, on_device(): query_sum = add_one(lax.all_gather(w_query, 'ctx', axis=0, tiled=True))  72.9 us
    ppermute x6, waiting for transfers between devices, from_behind(): return lax.ppermute(block, axis, route)  34.1 us
    ppermute x6, starting transfers between devices, from_behind(): return lax.ppermute(block, axis, route)  31.2 us
    dot_general x3, matrix products, fold_rows(): return jnp.dot(tokens, piece, preferred_element_type=jnp.float32)  13.1 us
  transfers between devices with their start and end apart: 9, of which 8 were waited for; matrix products, arithmetic and copies ran while one was open for 4% of the time, Pallas kernels for 0%

commit v1 on v0

v1 whole, which is shorter than its diff:
```python
import jax
import jax.numpy as jnp
from jax import lax
from jax.sharding import Mesh
from jax.sharding import PartitionSpec as P

WINDOW = 1024
PLANE = ("y", "x")
CTX = ("y", "x", "zh")
HEAD = ("zl", "core")

query_scale = 168.0 ** (-0.5)


def normalize(values, gain):
    return values * lax.rsqrt(jnp.mean(values * values, axis=-1, keepdims=True) + 1e-06) * gain


def rotate(values, position):
    half = values.shape[-1] // 2
    expo = jnp.arange(half, dtype=jnp.float32) * (2.0 / values.shape[-1])
    freq = jnp.power(jnp.float32(10000.0), -expo)
    angle = position[:, None] * freq[None, :]
    cosine = jnp.cos(angle)[:, None, :]
    sine = jnp.sin(angle)[:, None, :]
    first = values[..., :half]
    second = values[..., half:]
    return jnp.concatenate(
        [first * cosine - second * sine, second * cosine + first * sine], axis=-1
    )


def from_behind(block, distance):
    count = lax.axis_size(CTX)
    return lax.ppermute(block, CTX, [(i - distance, i) for i in range(distance, count)])


def on_device(tokens, w_query, key_weight, value_weight, query_gain, key_gain):
    row_count = tokens.shape[0]
    head_size = query_gain.shape[0]
    plane = lax.axis_size(PLANE)
    q_width = w_query.shape[1]
    kv_width = 2 * head_size

    mine = jnp.concatenate([key_weight, value_weight, w_query], axis=1)
    pair = lax.all_gather(mine, "zh", axis=0, tiled=True)
    pair_kv = pair[:, :kv_width]
    pair_q = pair[:, kv_width:]
    all_q = lax.all_gather(pair_q, PLANE, axis=0, tiled=True)
    all_kv = lax.all_to_all(
        jnp.broadcast_to(pair_kv[None], (plane,) + pair_kv.shape), PLANE, 0, 0, tiled=True
    ).reshape(-1, kv_width)

    offset = lax.axis_index(CTX) * row_count
    local_pos = offset + jnp.arange(row_count, dtype=jnp.int32)
    position = local_pos.astype(jnp.float32)

    kv_sum = jnp.dot(tokens, all_kv, preferred_element_type=jnp.float32)
    keys = rotate(normalize(kv_sum[:, None, :head_size], key_gain), position)[:, 0]
    kv = jnp.concatenate(
        [keys.astype(jnp.bfloat16), kv_sum[:, head_size:].astype(jnp.bfloat16)], axis=1
    )
    reach = WINDOW - 1
    hop_count = (reach + row_count - 1) // row_count
    needed = [min(row_count, reach - distance * row_count) for distance in range(hop_count)]
    sizes = [-(-rows // 16) * 16 for rows in needed]
    received = [
        from_behind(kv[row_count - size :], distance + 1) for distance, size in enumerate(sizes)
    ]
    before = sum(sizes)
    all_keys_values = jnp.concatenate(received[::-1] + [kv], axis=0)
    key_pos = offset - before + jnp.arange(before + row_count, dtype=jnp.int32)

    query_sum = jnp.dot(tokens, all_q, preferred_element_type=jnp.float32)
    queries = rotate(
        normalize(query_sum.reshape(row_count, 2, head_size), query_gain), position
    ).astype(jnp.bfloat16)

    allowed = (
        (key_pos[None, :] <= local_pos[:, None])
        & (key_pos[None, :] > local_pos[:, None] - WINDOW)
        & (key_pos[None, :] >= 0)
    )
    scores = (
        jnp.einsum(
            "bgd,cd->gbc",
            queries,
            all_keys_values[:, :head_size],
            preferred_element_type=jnp.float32,
        )
        * query_scale
    )
    scores = jnp.where(allowed[None], scores, jnp.float32(-1e30))
    top = jnp.max(scores, axis=-1, keepdims=True)
    weights = jnp.exp(scores - top)
    probs = (weights / jnp.sum(weights, axis=-1, keepdims=True)).astype(jnp.bfloat16)
    mixed = jnp.einsum(
        "gbc,cd->bgd", probs, all_keys_values[:, head_size:], preferred_element_type=jnp.float32
    )
    return mixed.reshape(row_count, q_width).astype(jnp.bfloat16)


def solution(mesh):
    split = Mesh(mesh.devices.reshape(4, 4, 2, 8, 2), CTX + HEAD)
    placed = (P(CTX, None), P(CTX, HEAD), P(CTX, HEAD), P(CTX, HEAD), P(), P())
    return jax.shard_map(
        on_device, mesh=split, in_specs=placed, out_specs=P(CTX, HEAD), check_vma=False
    )
```

time: 407 us -> 149 us (0.37)
  the two profiles are of different devices: /device:TPU:2 before, /device:TPU:50 now
where the time goes in v1:
time: 149 us
  waiting for transfers between devices  53.9 us (36%)
  starting transfers between devices  30.1 us (20%)
  blocking collectives  27.9 us (19%)
  matrix products  14.5 us (10%)
  between operations  13.6 us (9%)
  other arithmetic  5.06 us (3%)
  local copies, waits for them, and re-layouts  3.53 us (2%)
    all_to_all x1, waiting for transfers between devices, on_device(): lax.all_to_all(jnp.broadcast_to(pair_kv[None], (plane,) + pair_kv.shape),...  36 us
    all_gather x1, blocking collectives, on_device(): pair = lax.all_gather(mine, 'zh', axis=0, tiled=True)  27.9 us
    ppermute x3, starting transfers between devices, from_behind(): lax.ppermute(block, CTX, [(i - distance, i) for i in range(distance, coun...  22.8 us
    ppermute x3, waiting for transfers between devices, from_behind(): lax.ppermute(block, CTX, [(i - distance, i) for i in range(distance, coun...  17.8 us
    all_to_all x1, starting transfers between devices, on_device(): lax.all_to_all(jnp.broadcast_to(pair_kv[None], (plane,) + pair_kv.shape),...  7.25 us
    dot_general x1, matrix products, on_device(): query_sum = jnp.dot(tokens, all_q, preferred_element_type=jnp.float32)  4.65 us
    dot_general x1, matrix products, on_device(): kv_sum = jnp.dot(tokens, all_kv, preferred_element_type=jnp.float32)  3.78 us
    dot_general x1, matrix products, on_device(): jnp.einsum('gbc,cd->bgd', probs, all_keys_values[:, head_size:], preferre...  3.76 us
  transfers between devices with their start and end apart: 5, of which 2 were waited for; matrix products, arithmetic and copies ran while one was open for 6% of the time, Pallas kernels for 0%

profile of v1, /device:TPU:50, one launch (start us, length us, event | category | flops | bytes accessed | tf_op | source)
XLA Modules:
  0.0 148.6 jit_solution(11865930825600269100)
XLA Ops:
  6.5 0.0 all-gather.2.cloned.1.call-start
  6.5 0.9 pad_maximum_fusion.2
  7.5 27.9 %all_gather.6 = bf16[336,512]{1,0:T(8,128)(2,1)S(1)} all-gather(bf16[168,512]{1,0:T(8,128)(2,1)S(1)} %pad_maximum_fusion.2), channel_id=1, replica_groups=mesh['y'=4,'x'=4,'zh'=2,'zl'=8,'core'=2] {'zh'}, dimensions={0}, use_global_device_ids=true | all-gather | bytes 516096 | tf_op jit(solution)/shard_map/all_gather | solution.py:46
  35.4 0.7 fusion.30
  36.1 0.0 all-gather.2.cloned.1.call-update
  36.1 1.7 %broadcast_in_dim.10 = bf16[16,336,256]{2,1,0:T(8,128)(2,1)} broadcast(bf16[336,256]{1,0:T(8,128)(2,1)S(1)} %get-tuple-element.8), dimensions={1,2} | broadcast | bytes 2924544 | tf_op jit(solution)/shard_map/broadcast_in_dim | solution.py:51
  37.8 7.3 %all-to-all-start = ((bf16[16,336,256]{2,1,0:T(8,128)(2,1)}), bf16[16,336,256]{2,1,0:T(8,128)(2,1)S(1)}, u32[]{:S(2)}, u32[]{:S(2)}) async-start(bf16[16,336,256]{2,1,0:T(8,128)(2,1)} %broadcast_in_dim.10), calls=%async_computation | async-start | bytes 5505024 | tf_op jit(solution)/shard_map/all_to_all | solution.py:50
  45.1 0.7 and_and_fusion
  45.8 36.0 %all-to-all-done = bf16[16,336,256]{2,1,0:T(8,128)(2,1)S(1)} async-done(((bf16[16,336,256]{2,1,0:T(8,128)(2,1)}), bf16[16,336,256]{2,1,0:T(8,128)(2,1)S(1)}, u32[]{:S(2)}, u32[]{:S(2)}) %all-to-all-start) | async-done | bytes 2752544 | tf_op jit(solution)/shard_map/all_to_all | solution.py:50
  81.8 0.0 copy-start.1
  81.8 3.8 %convolution_bitcast_fusion = f32[448,256]{1,0:T(8,128)S(1)} fusion(bf16[448,5376]{1,0:T(8,128)(2,1)} %param.6, bf16[5376,256]{1,0:T(8,128)(2,1)S(1)} %bitcast.52), kind=kOutput, calls=%fused_computation.10 | convolution fusion | flops 1233125376 | bytes 8028160 | tf_op jit(solution)/shard_map/dot_general | solution.py:58
  85.7 0.1 multiply_reduce_fusion.1
  85.8 0.0 copy-done.1
  85.8 0.1 multiply_bitcast_fusion
  86.0 1.1 fusion.17
  87.1 0.1 maximum_bitcast_fusion
  87.2 3.3 %collective-permute-start.1 = (bf16[448,256]{1,0:T(8,128)(2,1)S(1)}, bf16[448,256]{1,0:T(8,128)(2,1)S(1)}, u32[]{:S(2)}, u32[]{:S(2)}) collective-permute-start(bf16[448,256]{1,0:T(8,128)(2,1)S(1)} %pad_maximum_fusion), channel_id=1, source_target_pairs={{0,32},{16,48},{32,64},{48,80},{64,96},{80,112},{96,128},{112,144}... | collective-permute-start | bytes 688136 | tf_op jit(solution)/shard_map/ppermute | solution.py:35
  90.5 12.5 %collective-permute-start.2 = (bf16[448,256]{1,0:T(8,128)(2,1)S(1)}, bf16[448,256]{1,0:T(8,128)(2,1)S(1)}, u32[]{:S(2)}, u32[]{:S(2)}) collective-permute-start(bf16[448,256]{1,0:T(8,128)(2,1)S(1)} %pad_maximum_fusion), channel_id=1, source_target_pairs={{0,16},{16,32},{32,48},{48,64},{64,80},{80,96},{96,112},{112,128},... | collective-permute-start | bytes 688136 | tf_op jit(solution)/shard_map/ppermute | solution.py:35
  103.1 7.0 %collective-permute-start = (bf16[128,256]{1,0:T(8,128)(2,1)S(1)}, bf16[128,256]{1,0:T(8,128)(2,1)S(1)}, u32[]{:S(2)}, u32[]{:S(2)}) collective-permute-start(bf16[128,256]{1,0:T(8,128)(2,1)S(1)} %fusion.20), channel_id=1, source_target_pairs={{0,48},{16,64},{32,80},{48,96},{64,112},{80,128},{96,144},{112,160... | collective-permute-start | bytes 196616 | tf_op jit(solution)/shard_map/ppermute | solution.py:35
  110.1 0.9 multiply_cosine_fusion
  111.0 17.8 %collective-permute-done = bf16[128,256]{1,0:T(8,128)(2,1)S(1)} collective-permute-done((bf16[128,256]{1,0:T(8,128)(2,1)S(1)}, bf16[128,256]{1,0:T(8,128)(2,1)S(1)}, u32[]{:S(2)}, u32[]{:S(2)}) %collective-permute-start) | collective-permute-done | bytes 65568 | tf_op jit(solution)/shard_map/ppermute | solution.py:35
  128.8 0.0 collective-permute-done.1
  128.8 0.0 collective-permute-done.2
  128.8 0.1 maximum_maximum_fusion
  128.9 0.0 copy-start
  128.9 0.0 all-gather.2.cloned.1.call-done
  128.9 4.7 %fusion.32 = f32[256,448]{0,1:T(8,128)S(1)} fusion(bf16[448,5376]{1,0:T(8,128)(2,1)} %param.6, bf16[5376,256]{1,0:T(8,128)(2,1)} %all-gather.2.cloned.1.call-done), kind=kOutput, calls=%fused_computation.61 | convolution fusion | flops 1233125376 | bytes 8028160 | tf_op jit(solution)/shard_map/dot_general | solution.py:74
  133.6 0.2 reshape.229
  133.8 0.5 multiply_reduce_fusion
  134.4 0.1 copy.13
  134.5 0.0 copy-done
  134.5 0.2 fusion.10
  134.7 0.2 subtract_convert_fusion
  134.9 2.3 %fusion.31 = f32[2,448]{1,0:T(2,128)S(1)} fusion(pred[448,1472]{1,0:T(8,128)(4,1)S(1)} %and_and_fusion, bf16[1472,256]{1,0:T(8,128)(2,1)S(1)} %maximum_maximum_fusion, bf16[448,2,64]{2,0,1:T(8,128)(2,1)S(1)} %get-tuple-element.6, bf16[448,2,64]{2,0,1:T(8,128)(2,1)S(1)} %get-tuple-element.5), kind=kOutput, calls=%fused_computation.60 | convolution fusion | flops 343377344 | bytes 1527296 | tf_op jit(solution)/shard_map/sub | solution.py:95
  137.2 3.8 %fusion.7 = bf16[2,56,8,128]{3,2,1,0:T(8,128)(2,1)S(1)} fusion(f32[2,448]{1,0:T(2,128)S(1)} %fusion.31, bf16[1472,256]{1,0:T(8,128)(2,1)S(1)} %maximum_maximum_fusion, pred[448,1472]{1,0:T(8,128)(4,1)S(1)} %and_and_fusion, bf16[448,2,64]{2,0,1:T(8,128)(2,1)S(1)} %get-tuple-element.6, bf16[448,2,64]{2,0,1:T(8,128)(2,1)S(1)} %get-tuple-element.5), kind=kOutput, calls=%fused_computation.12 | convolution fusion | flops 682453312 | bytes 1875456 | tf_op jit(solution)/shard_map/gbc,cd->bgd/dot_general | solution.py:97
  141.0 0.7 copy.20
  (10 shorter events, 0.1 us)
Async XLA Ops:
  6.5 122.4 %all-gather.2.cloned.1.call-start = ((), (), s32[]{:S(2)}) async-start(), calls=%async_computation.1 | async-start | bytes 2924544 | tf_op jit(solution)/shard_map/all_gather | solution.py:49
  37.8 44.0 %all-to-all-start = ((bf16[16,336,256]{2,1,0:T(8,128)(2,1)}), bf16[16,336,256]{2,1,0:T(8,128)(2,1)S(1)}, u32[]{:S(2)}, u32[]{:S(2)}) async-start(bf16[16,336,256]{2,1,0:T(8,128)(2,1)} %broadcast_in_dim.10), calls=%async_computation | async-start | bytes 5505024 | tf_op jit(solution)/shard_map/all_to_all | solution.py:50
  81.8 4.0 %copy-start.1 = (f32[128]{0:T(128)S(1)}, f32[128]{0:T(128)}, u32[]{:S(2)}) copy-start(f32[128]{0:T(128)} %param.11) | copy-start | bytes 1540
  87.2 41.6 %collective-permute-start.1 = (bf16[448,256]{1,0:T(8,128)(2,1)S(1)}, bf16[448,256]{1,0:T(8,128)(2,1)S(1)}, u32[]{:S(2)}, u32[]{:S(2)}) collective-permute-start(bf16[448,256]{1,0:T(8,128)(2,1)S(1)} %pad_maximum_fusion), channel_id=1, source_target_pairs={{0,32},{16,48},{32,64},{48,80},{64,96},{80,112},{96,128},{112,144}... | collective-permute-start | bytes 688136 | tf_op jit(solution)/shard_map/ppermute | solution.py:35
  90.5 38.3 %collective-permute-start.2 = (bf16[448,256]{1,0:T(8,128)(2,1)S(1)}, bf16[448,256]{1,0:T(8,128)(2,1)S(1)}, u32[]{:S(2)}, u32[]{:S(2)}) collective-permute-start(bf16[448,256]{1,0:T(8,128)(2,1)S(1)} %pad_maximum_fusion), channel_id=1, source_target_pairs={{0,16},{16,32},{32,48},{48,64},{64,80},{80,96},{96,112},{112,128},... | collective-permute-start | bytes 688136 | tf_op jit(solution)/shard_map/ppermute | solution.py:35
  103.1 25.7 %collective-permute-start = (bf16[128,256]{1,0:T(8,128)(2,1)S(1)}, bf16[128,256]{1,0:T(8,128)(2,1)S(1)}, u32[]{:S(2)}, u32[]{:S(2)}) collective-permute-start(bf16[128,256]{1,0:T(8,128)(2,1)S(1)} %fusion.20), channel_id=1, source_target_pairs={{0,48},{16,64},{32,80},{48,96},{64,112},{80,128},{96,144},{112,160... | collective-permute-start | bytes 196616 | tf_op jit(solution)/shard_map/ppermute | solution.py:35
  128.9 5.6 %copy-start = (f32[128]{0:T(128)S(1)}, f32[128]{0:T(128)}, u32[]{:S(2)}) copy-start(f32[128]{0:T(128)} %param.10) | copy-start | bytes 1540
Sparse Core Ops, SparseCore 0:
  36.2 82.0 all-gather.1

commit v2 on v1

v2 whole, which is shorter than its diff:
```python
import itertools

import jax
import jax.numpy as jnp
from jax import lax
from jax.experimental import pallas as pl
from jax.experimental.pallas import tpu as pltpu
from jax.sharding import Mesh
from jax.sharding import PartitionSpec as P

WINDOW = 1024
SIDE = 4
CTX = ("y", "x", "zh")
HEAD = ("zl", "core")
QUERY_BLOCK = 64

query_scale = 168.0 ** (-0.5)


def rings(stage):
    groups = []
    for zh, zl, core in itertools.product(range(2), range(8), range(2)):
        for fixed in range(SIDE):
            places = [(fixed, i) if core == stage else (i, fixed) for i in range(SIDE)]
            groups.append([(((y * SIDE + x) * 2 + zh) * 8 + zl) * 2 + core for y, x in places])
    return groups


def round_ring(block, stage):
    sent = jnp.broadcast_to(block[None], (SIDE,) + block.shape)
    return lax.all_to_all(sent, CTX + HEAD, 0, 0, tiled=True, axis_index_groups=rings(stage))


def from_behind(block, distance):
    count = lax.axis_size(CTX)
    return lax.ppermute(block, CTX, [(i - distance, i) for i in range(distance, count)])


def rotary_tables(position, head_size):
    half = head_size // 2
    expo = jnp.arange(half, dtype=jnp.float32) * (2.0 / head_size)
    freq = jnp.power(jnp.float32(10000.0), -expo)
    angle = position[:, None] * freq[None, :]
    cosine = jnp.cos(angle)
    sine = jnp.sin(angle)
    return jnp.concatenate([cosine, cosine], 1), jnp.concatenate([-sine, sine], 1)


def projection(tokens, weight, gain, cosine, sine, core, normed_heads):
    row_count, width = tokens.shape
    columns = weight.shape[-1]
    head_size = gain.shape[-1]
    block = weight.shape[-2]
    weight = weight.reshape(SIDE * SIDE, block, columns)

    def body(core_ref, tokens_ref, weight_ref, gain_ref, cosine_ref, sine_ref, out_ref, rows_ref):
        first = core_ref[0] == 0
        for y, x in itertools.product(range(SIDE), range(SIDE)):
            place = y * SIDE + x
            source = jnp.where(first, place, x * SIDE + y)
            rows_ref[place * block : (place + 1) * block, :] = weight_ref[source]
        total = jnp.dot(tokens_ref[...], rows_ref[...], preferred_element_type=jnp.float32)
        for head in range(columns // head_size):
            span = slice(head * head_size, (head + 1) * head_size)
            values = total[:, span]
            if head < normed_heads:
                mean = jnp.mean(values * values, axis=-1, keepdims=True)
                values = values * lax.rsqrt(mean + 1e-06) * gain_ref[...]
                turned = pltpu.roll(values, head_size // 2, 1)
                values = values * cosine_ref[...] + turned * sine_ref[...]
            out_ref[:, span] = values.astype(out_ref.dtype)

    whole = pl.BlockSpec(memory_space=pltpu.VMEM)
    return pl.pallas_call(
        body,
        out_shape=jax.ShapeDtypeStruct((row_count, columns), jnp.bfloat16),
        in_specs=[pl.BlockSpec(memory_space=pltpu.SMEM)] + [whole] * 5,
        out_specs=whole,
        scratch_shapes=[pltpu.VMEM((width, columns), jnp.bfloat16)],
        compiler_params=pltpu.CompilerParams(vmem_limit_bytes=40 << 20),
        cost_estimate=pl.CostEstimate(
            flops=2 * row_count * width * columns,
            transcendentals=0,
            bytes_accessed=2 * width * (row_count + columns),
        ),
        name="projection",
    )(core, tokens, weight, gain.reshape(1, -1), cosine, sine)


def attention(queries, pieces, offset):
    row_count, q_width = queries.shape
    head_size = pieces[0].shape[1] // 2
    heads = q_width // head_size
    sizes = [piece.shape[0] for piece in pieces]
    before = sum(sizes[:-1])
    reach = before + QUERY_BLOCK

    def body(offset_ref, queries_ref, *refs):
        piece_refs, out_ref, all_ref = refs[:-2], refs[-2], refs[-1]
        start = 0
        for piece_ref, size in zip(piece_refs, sizes):
            all_ref[start : start + size, :] = piece_ref[...]
            start += size
        shape = (heads, QUERY_BLOCK, reach)
        row = lax.broadcasted_iota(jnp.int32, shape, 1).reshape(heads * QUERY_BLOCK, reach)
        column = lax.broadcasted_iota(jnp.int32, shape, 2).reshape(heads * QUERY_BLOCK, reach)
        lag = row + before - column
        in_window = (lag >= 0) & (lag < WINDOW)
        for first in range(0, row_count, QUERY_BLOCK):
            rows = slice(first, first + QUERY_BLOCK)
            keys = all_ref[first : first + reach, :head_size]
            values = all_ref[first : first + reach, head_size:]
            block = jnp.concatenate(
                [
                    queries_ref[rows, head * head_size : (head + 1) * head_size]
                    for head in range(heads)
                ],
                axis=0,
            )
            scores = lax.dot_general(
                block, keys, (((1,), (1,)), ((), ())), preferred_element_type=jnp.float32
            )
            allowed = in_window & (column >= before - first - offset_ref[0])
            scores = jnp.where(allowed, scores * query_scale, jnp.float32(-1e30))
            top = jnp.max(scores, axis=-1, keepdims=True)
            weights = jnp.exp(scores - top)
            total = jnp.sum(weights, axis=-1, keepdims=True)
            mixed = jnp.dot(
                weights.astype(jnp.bfloat16), values, preferred_element_type=jnp.float32
            )
            mixed = mixed / total
            for head in range(heads):
                out_ref[rows, head * head_size : (head + 1) * head_size] = mixed[
                    head * QUERY_BLOCK : (head + 1) * QUERY_BLOCK
                ].astype(out_ref.dtype)

    whole = pl.BlockSpec(memory_space=pltpu.VMEM)
    return pl.pallas_call(
        body,
        out_shape=jax.ShapeDtypeStruct((row_count, q_width), jnp.bfloat16),
        in_specs=[pl.BlockSpec(memory_space=pltpu.SMEM)] + [whole] * (1 + len(pieces)),
        out_specs=whole,
        scratch_shapes=[pltpu.VMEM((before + row_count, 2 * head_size), jnp.bfloat16)],
        compiler_params=pltpu.CompilerParams(vmem_limit_bytes=32 << 20),
        cost_estimate=pl.CostEstimate(
            flops=4 * row_count * q_width * reach,
            transcendentals=row_count * heads * reach,
            bytes_accessed=4 * (row_count * q_width + (before + row_count) * head_size),
        ),
        name="attention",
    )(offset.reshape(1), queries, *pieces)


def on_device(tokens, w_query, key_weight, value_weight, query_gain, key_gain):
    row_count = tokens.shape[0]
    head_size = query_gain.shape[0]
    kv_width = 2 * head_size
    low = lax.axis_index("zh") == 0
    core = lax.axis_index("core").astype(jnp.int32).reshape(1)

    mine = jnp.concatenate([key_weight, value_weight, w_query], axis=1)
    other = lax.ppermute(mine, "zh", [(0, 1), (1, 0)])
    pair = jnp.where(
        low, jnp.concatenate([mine, other], axis=0), jnp.concatenate([other, mine], axis=0)
    )
    line = round_ring(pair, 0)
    all_kv = round_ring(line[:, :, :kv_width], 1)
    line_q, all_kv = lax.optimization_barrier((line[:, :, kv_width:], all_kv))
    all_q = round_ring(line_q, 1)

    offset = (lax.axis_index(CTX) * row_count).astype(jnp.int32)
    position = (offset + jnp.arange(row_count, dtype=jnp.int32)).astype(jnp.float32)
    cosine, sine = rotary_tables(position, head_size)

    kv = projection(tokens, all_kv, key_gain, cosine, sine, core, 1)
    reach = WINDOW - 1
    hop_count = (reach + row_count - 1) // row_count
    needed = [min(row_count, reach - distance * row_count) for distance in range(hop_count)]
    sizes = [-(-rows // 16) * 16 for rows in needed]
    received = [
        from_behind(kv[row_count - size :], distance + 1) for distance, size in enumerate(sizes)
    ]
    queries = projection(tokens, all_q, query_gain, cosine, sine, core, 2)
    return attention(queries, received[::-1] + [kv], offset)


def solution(mesh):
    split = Mesh(mesh.devices.reshape(SIDE, SIDE, 2, 8, 2), CTX + HEAD)
    placed = (P(CTX, None), P(CTX, HEAD), P(CTX, HEAD), P(CTX, HEAD), P(), P())
    return jax.shard_map(
        on_device, mesh=split, in_specs=placed, out_specs=P(CTX, HEAD), check_vma=False
    )
```

time: 149 us -> 130 us (0.87)
  the two profiles are of different devices: /device:TPU:50 before, /device:TPU:112 now
where the time goes in v2:
time: 130 us
  starting transfers between devices  42.1 us (32%)
  blocking collectives  41.8 us (32%)
  waiting for transfers between devices  24.3 us (19%)
  local copies, waits for them, and re-layouts  11.7 us (9%)
  Pallas kernels  8.39 us (6%)
    all_to_all x2, blocking collectives, round_ring(): lax.all_to_all(sent, CTX + HEAD, 0, 0, tiled=True, axis_index_groups=ring...  41.8 us
    ppermute x3, starting transfers between devices, from_behind(): lax.ppermute(block, CTX, [(i - distance, i) for i in range(distance, coun...  22.6 us
    ppermute x1, starting transfers between devices, on_device(): other = lax.ppermute(mine, 'zh', [(0, 1), (1, 0)])  13 us
    ppermute x3, waiting for transfers between devices, from_behind(): lax.ppermute(block, CTX, [(i - distance, i) for i in range(distance, coun...  12.6 us
    ppermute x1, waiting for transfers between devices, on_device(): other = lax.ppermute(mine, 'zh', [(0, 1), (1, 0)])  11.7 us
    unnamed x12, local copies, waits for them, and re-layouts  8.09 us
    all_to_all x1, starting transfers between devices, round_ring(): lax.all_to_all(sent, CTX + HEAD, 0, 0, tiled=True, axis_index_groups=ring...  6.48 us
    pallas_call x1, Pallas kernels, attention(): pl.pallas_call(body, out_shape=jax.ShapeDtypeStruct((row_count, q_width),...  4.69 us
  transfers between devices with their start and end apart: 5, of which 2 were waited for; matrix products, arithmetic and copies ran while one was open for 1% of the time, Pallas kernels for 3%

profile of v2, /device:TPU:112, one launch (start us, length us, event | category | flops | bytes accessed | tf_op | source)
XLA Modules:
  0.0 129.7 jit_solution(719722888805090125)
XLA Ops:
  0.0 0.8 constant_dynamic-update-slice_fusion.2
  0.8 0.8 constant_dynamic-update-slice_fusion.1
  1.6 0.9 constant_dynamic-update-slice_fusion
  2.5 13.0 %collective-permute-start = (bf16[168,512]{1,0:T(8,128)(2,1)S(1)}, bf16[168,512]{1,0:T(8,128)(2,1)S(1)}, u32[]{:S(2)}, u32[]{:S(2)}) collective-permute-start(bf16[168,512]{1,0:T(8,128)(2,1)S(1)} %constant_dynamic-update-slice_fusion), channel_id=1, source_target_pairs={{0,16},{16,0},{1,17},{17,1},{2,18},{18,2},{3,19},{19,3},{4,20},{20... | collective-permute-start | bytes 516104 | tf_op jit(solution)/shard_map/ppermute | solution.py:162
  15.5 11.7 %collective-permute-done = bf16[168,512]{1,0:T(8,128)(2,1)S(1)} collective-permute-done((bf16[168,512]{1,0:T(8,128)(2,1)S(1)}, bf16[168,512]{1,0:T(8,128)(2,1)S(1)}, u32[]{:S(2)}, u32[]{:S(2)}) %collective-permute-start) | collective-permute-done | bytes 172064 | tf_op jit(solution)/shard_map/ppermute | solution.py:162
  27.2 0.1 maximum_select_fusion
  27.3 0.1 broadcast_in_dim.6
  27.5 19.8 %all_to_all.15 = bf16[4,336,512]{2,1,0:T(8,128)(2,1)S(1)} all-to-all(bf16[4,336,512]{2,1,0:T(8,128)(2,1)S(1)} %broadcast_in_dim.6), channel_id=1, replica_groups={{0,32,64,96},{128,160,192,224},{256,288,320,352},{384,416,448,480},{1,1..., dimensions={0} | all-to-all | bytes 2752512 | tf_op jit(solution)/shard_map/all_to_all | solution.py:31
  47.3 0.1 fusion.1
  47.4 0.2 broadcast_in_dim.7
  47.6 22.0 %all_to_all.16 = bf16[4,4,336,256]{3,2,1,0:T(8,128)(2,1)} all-to-all(bf16[4,4,336,256]{3,2,1,0:T(8,128)(2,1)S(1)} %broadcast_in_dim.7), channel_id=1, replica_groups={{0,128,256,384},{32,160,288,416},{64,192,320,448},{96,224,352,480},{1,3..., dimensions={0} | all-to-all | bytes 5505024 | tf_op jit(solution)/shard_map/all_to_all | solution.py:31
  69.6 1.7 %broadcast_in_dim.8 = bf16[4,4,336,256]{3,2,1,0:T(8,128)(2,1)} broadcast(bf16[4,336,256]{2,1,0:T(8,128)(2,1)S(1)} %get-tuple-element.7), dimensions={1,2,3} | broadcast | bytes 3440640 | tf_op jit(solution)/shard_map/broadcast_in_dim | solution.py:30
  71.3 0.0 copy-start.3
  71.3 6.5 %all-to-all-start.2 = ((bf16[4,4,336,256]{3,2,1,0:T(8,128)(2,1)}), bf16[4,4,336,256]{3,2,1,0:T(8,128)(2,1)S(1)}, u32[]{:S(2)}, u32[]{:S(2)}) async-start(bf16[4,4,336,256]{3,2,1,0:T(8,128)(2,1)} %broadcast_in_dim.8), calls=%async_computation.2 | async-start | bytes 5505024 | tf_op jit(solution)/shard_map/all_to_all | solution.py:31
  77.8 0.9 fusion
  78.7 0.2 pad_maximum_fusion
  78.9 0.0 copy-done.3
  78.9 0.0 copy-start
  78.9 2.4 %copy-done = bf16[448,5376]{1,0:T(8,128)(2,1)S(1)} copy-done((bf16[448,5376]{1,0:T(8,128)(2,1)S(1)}, bf16[448,5376]{1,0:T(8,128)(2,1)}, u32[]{:S(2)}) %copy-start) | copy-done | bytes 4816920
  81.2 0.0 copy-start.2
  81.2 1.8 %copy-done.2 = bf16[4,4,336,256]{3,2,1,0:T(8,128)(2,1)S(1)} copy-done((bf16[4,4,336,256]{3,2,1,0:T(8,128)(2,1)S(1)}, bf16[4,4,336,256]{3,2,1,0:T(8,128)(2,1)}, u32[]{:S(2)}) %copy-start.2) | copy-done | bytes 2752536
  83.0 0.0 copy-start.4
  83.0 1.7 %projection.3.refs_3_ = bf16[448,256]{1,0:T(8,128)(2,1)S(1)} custom-call(s32[1]{0:T(128)} %bitcast.1.core_ref, bf16[448,5376]{1,0:T(8,128)(2,1)S(1)} %copy-done, bf16[16,336,256]{2,1,0:T(8,128)(2,1)S(1)} %bitcast.7, f32[1,128]{1,0:T(1,128)S(1)} %bitcast.8, f32[448,128]{1,0:T(8,128)S(1)} %get-tuple-element.14.cosine_ref, ...), custom_call_target="tpu_custom_call" | custom-call | flops 1233125376 | bytes 7569408 | tf_op jit(solution)/shard_map/projection/pallas_call | solution.py:74
  84.8 18.2 %collective-permute-start.3 = (bf16[448,256]{1,0:T(8,128)(2,1)S(1)}, bf16[448,256]{1,0:T(8,128)(2,1)}, u32[]{:S(2)}, u32[]{:S(2)}) collective-permute-start(bf16[448,256]{1,0:T(8,128)(2,1)S(1)} %projection.3.refs_3_), channel_id=1, source_target_pairs={{0,16},{16,32},{32,48},{48,64},{64,80},{80,96},{96,112},{112,128},... | collective-permute-start | bytes 688136 | tf_op jit(solution)/shard_map/ppermute | solution.py:36
  103.0 2.5 %collective-permute-start.2 = (bf16[448,256]{1,0:T(8,128)(2,1)S(1)}, bf16[448,256]{1,0:T(8,128)(2,1)}, u32[]{:S(2)}, u32[]{:S(2)}) collective-permute-start(bf16[448,256]{1,0:T(8,128)(2,1)S(1)} %projection.3.refs_3_), channel_id=1, source_target_pairs={{0,32},{16,48},{32,64},{48,80},{64,96},{80,112},{96,128},{112,144}... | collective-permute-start | bytes 688136 | tf_op jit(solution)/shard_map/ppermute | solution.py:36
  105.4 0.6 slice.14
  106.1 1.9 %collective-permute-start.1 = (bf16[128,256]{1,0:T(8,128)(2,1)}, bf16[128,256]{1,0:T(8,128)(2,1)S(1)}, u32[]{:S(2)}, u32[]{:S(2)}) collective-permute-start(bf16[128,256]{1,0:T(8,128)(2,1)} %slice.14), channel_id=1, source_target_pairs={{0,48},{16,64},{32,80},{48,96},{64,112},{80,128},{96,144},{112,160... | collective-permute-start | bytes 196616 | tf_op jit(solution)/shard_map/ppermute | solution.py:36
  108.0 0.0 all-to-all-done.2
  108.0 0.0 copy-done.4
  108.0 0.0 copy-start.1
  108.0 2.4 %copy-done.1 = bf16[448,5376]{1,0:T(8,128)(2,1)S(1)} copy-done((bf16[448,5376]{1,0:T(8,128)(2,1)S(1)}, bf16[448,5376]{1,0:T(8,128)(2,1)}, u32[]{:S(2)}) %copy-start.1) | copy-done | bytes 4816920
  110.4 2.0 %projection.2.queries_ref = bf16[448,256]{1,0:T(8,128)(2,1)S(1)} custom-call(s32[1]{0:T(128)} %bitcast.1.core_ref, bf16[448,5376]{1,0:T(8,128)(2,1)S(1)} %copy-done.1, bf16[16,336,256]{2,1,0:T(8,128)(2,1)S(1)} %bitcast.6, f32[1,128]{1,0:T(1,128)S(1)} %bitcast.9, f32[448,128]{1,0:T(8,128)S(1)} %get-tuple-element.14.cosine_ref, ...), custom_call_target="tpu_custom_call" | custom-call | flops 1233125376 | bytes 7569408 | tf_op jit(solution)/shard_map/projection/pallas_call | solution.py:74
  112.4 12.6 %collective-permute-done.1.refs_0_ = bf16[128,256]{1,0:T(8,128)(2,1)S(1)} collective-permute-done((bf16[128,256]{1,0:T(8,128)(2,1)}, bf16[128,256]{1,0:T(8,128)(2,1)S(1)}, u32[]{:S(2)}, u32[]{:S(2)}) %collective-permute-start.1) | collective-permute-done | bytes 65568 | tf_op jit(solution)/shard_map/ppermute | solution.py:36
  125.0 0.0 collective-permute-done.3.refs_2_
  125.0 0.0 collective-permute-done.2.refs_1_
  125.0 4.7 %attention.1 = bf16[448,256]{1,0:T(8,128)(2,1)} custom-call(s32[1]{0:T(128)} %bitcast.offset_ref, bf16[448,256]{1,0:T(8,128)(2,1)S(1)} %projection.2.queries_ref, bf16[128,256]{1,0:T(8,128)(2,1)S(1)} %collective-permute-done.1.refs_0_, bf16[448,256]{1,0:T(8,128)(2,1)} %collective-permute-done.2.refs_1_, bf16[448,256]{1,0:T(8,128)(2,1)} %collective-permute-done.3.refs_2_, ...), custom_call_target="tpu_custom_call" | custom-call | flops 499122176 | bytes 1212416 | tf_op jit(solution)/shard_map/attention/pallas_call | solution.py:138
  (2 shorter events, 0.0 us)
Async XLA Ops:
  2.5 24.7 %collective-permute-start = (bf16[168,512]{1,0:T(8,128)(2,1)S(1)}, bf16[168,512]{1,0:T(8,128)(2,1)S(1)}, u32[]{:S(2)}, u32[]{:S(2)}) collective-permute-start(bf16[168,512]{1,0:T(8,128)(2,1)S(1)} %constant_dynamic-update-slice_fusion), channel_id=1, source_target_pairs={{0,16},{16,0},{1,17},{17,1},{2,18},{18,2},{3,19},{19,3},{4,20},{20... | collective-permute-start | bytes 516104 | tf_op jit(solution)/shard_map/ppermute | solution.py:162
  71.3 7.6 %copy-start.3 = (f32[128]{0:T(128)S(1)}, f32[128]{0:T(128)}, u32[]{:S(2)}) copy-start(f32[128]{0:T(128)} %param.11) | copy-start | bytes 1540
  71.3 36.7 %all-to-all-start.2 = ((bf16[4,4,336,256]{3,2,1,0:T(8,128)(2,1)}), bf16[4,4,336,256]{3,2,1,0:T(8,128)(2,1)S(1)}, u32[]{:S(2)}, u32[]{:S(2)}) async-start(bf16[4,4,336,256]{3,2,1,0:T(8,128)(2,1)} %broadcast_in_dim.8), calls=%async_computation.2 | async-start | bytes 5505024 | tf_op jit(solution)/shard_map/all_to_all | solution.py:31
  78.9 2.4 %copy-start = (bf16[448,5376]{1,0:T(8,128)(2,1)S(1)}, bf16[448,5376]{1,0:T(8,128)(2,1)}, u32[]{:S(2)}) copy-start(bf16[448,5376]{1,0:T(8,128)(2,1)} %tokens_ref.3) | copy-start | bytes 14450692
  81.2 1.8 %copy-start.2 = (bf16[4,4,336,256]{3,2,1,0:T(8,128)(2,1)S(1)}, bf16[4,4,336,256]{3,2,1,0:T(8,128)(2,1)}, u32[]{:S(2)}) copy-start(bf16[4,4,336,256]{3,2,1,0:T(8,128)(2,1)} %all_to_all.16) | copy-start | bytes 8257540
  83.0 25.0 %copy-start.4 = (f32[128]{0:T(128)S(1)}, f32[128]{0:T(128)}, u32[]{:S(2)}) copy-start(f32[128]{0:T(128)} %param.10) | copy-start | bytes 1540
  84.8 40.2 %collective-permute-start.3 = (bf16[448,256]{1,0:T(8,128)(2,1)S(1)}, bf16[448,256]{1,0:T(8,128)(2,1)}, u32[]{:S(2)}, u32[]{:S(2)}) collective-permute-start(bf16[448,256]{1,0:T(8,128)(2,1)S(1)} %projection.3.refs_3_), channel_id=1, source_target_pairs={{0,16},{16,32},{32,48},{48,64},{64,80},{80,96},{96,112},{112,128},... | collective-permute-start | bytes 688136 | tf_op jit(solution)/shard_map/ppermute | solution.py:36
  103.0 22.0 %collective-permute-start.2 = (bf16[448,256]{1,0:T(8,128)(2,1)S(1)}, bf16[448,256]{1,0:T(8,128)(2,1)}, u32[]{:S(2)}, u32[]{:S(2)}) collective-permute-start(bf16[448,256]{1,0:T(8,128)(2,1)S(1)} %projection.3.refs_3_), channel_id=1, source_target_pairs={{0,32},{16,48},{32,64},{48,80},{64,96},{80,112},{96,128},{112,144}... | collective-permute-start | bytes 688136 | tf_op jit(solution)/shard_map/ppermute | solution.py:36
  106.1 18.9 %collective-permute-start.1 = (bf16[128,256]{1,0:T(8,128)(2,1)}, bf16[128,256]{1,0:T(8,128)(2,1)S(1)}, u32[]{:S(2)}, u32[]{:S(2)}) collective-permute-start(bf16[128,256]{1,0:T(8,128)(2,1)} %slice.14), channel_id=1, source_target_pairs={{0,48},{16,64},{32,80},{48,96},{64,112},{80,128},{96,144},{112,160... | collective-permute-start | bytes 196616 | tf_op jit(solution)/shard_map/ppermute | solution.py:36
  108.0 2.4 %copy-start.1 = (bf16[448,5376]{1,0:T(8,128)(2,1)S(1)}, bf16[448,5376]{1,0:T(8,128)(2,1)}, u32[]{:S(2)}) copy-start(bf16[448,5376]{1,0:T(8,128)(2,1)} %tokens_ref.3) | copy-start | bytes 14450692

commit v3 on v2

--- a/solution.py
+++ b/solution.py
@@ -10,9 +10,11 @@
 
 WINDOW = 1024
 SIDE = 4
+SHIFTS = (0, 1, 3, 2)
 CTX = ("y", "x", "zh")
 HEAD = ("zl", "core")
 QUERY_BLOCK = 64
+COST = 10**10
 
 query_scale = 168.0 ** (-0.5)
 
@@ -31,6 +33,11 @@
     return lax.all_to_all(sent, CTX + HEAD, 0, 0, tiled=True, axis_index_groups=rings(stage))
 
 
+def along_ring(block, stage, distance):
+    pairs = [(ring[i - distance], ring[i]) for ring in rings(stage) for i in range(SIDE)]
+    return lax.ppermute(block, CTX + HEAD, pairs)
+
+
 def from_behind(block, distance):
     count = lax.axis_size(CTX)
     return lax.ppermute(block, CTX, [(i - distance, i) for i in range(distance, count)])
@@ -43,23 +50,30 @@
     angle = position[:, None] * freq[None, :]
     cosine = jnp.cos(angle)
     sine = jnp.sin(angle)
-    return jnp.concatenate([cosine, cosine], 1), jnp.concatenate([-sine, sine], 1)
-
-
-def projection(tokens, weight, gain, cosine, sine, core, normed_heads):
+    return jnp.stack(
+        [jnp.concatenate([cosine, cosine], 1), jnp.concatenate([-sine, sine], 1)]
+    )
+
+
+def projection(tokens, weight, order, gain, tables, normed_heads, tail=0):
     row_count, width = tokens.shape
     columns = weight.shape[-1]
     head_size = gain.shape[-1]
     block = weight.shape[-2]
     weight = weight.reshape(SIDE * SIDE, block, columns)
 
-    def body(core_ref, tokens_ref, weight_ref, gain_ref, cosine_ref, sine_ref, out_ref, rows_ref):
-        first = core_ref[0] == 0
-        for y, x in itertools.product(range(SIDE), range(SIDE)):
-            place = y * SIDE + x
-            source = jnp.where(first, place, x * SIDE + y)
-            rows_ref[place * block : (place + 1) * block, :] = weight_ref[source]
+    tables = pltpu.with_memory_space_constraint(tables, pltpu.HBM)
+
+    def body(order_ref, tokens_ref, weight_ref, gain_ref, tables_ref, *refs):
+        out_refs = refs[:-3]
+        out_ref = out_refs[0]
+        here_ref, rows_ref, sem = refs[-3:]
+        copy = pltpu.make_async_copy(tables_ref, here_ref, sem)
+        copy.start()
+        for place in range(SIDE * SIDE):
+            rows_ref[place * block : (place + 1) * block, :] = weight_ref[order_ref[place]]
         total = jnp.dot(tokens_ref[...], rows_ref[...], preferred_element_type=jnp.float32)
+        copy.wait()
         for head in range(columns // head_size):
             span = slice(head * head_size, (head + 1) * head_size)
             values = total[:, span]
@@ -67,24 +81,44 @@
                 mean = jnp.mean(values * values, axis=-1, keepdims=True)
                 values = values * lax.rsqrt(mean + 1e-06) * gain_ref[...]
                 turned = pltpu.roll(values, head_size // 2, 1)
-                values = values * cosine_ref[...] + turned * sine_ref[...]
+                values = values * here_ref[0] + turned * here_ref[1]
             out_ref[:, span] = values.astype(out_ref.dtype)
-
+        if tail:
+            out_refs[1][...] = out_ref[row_count - tail :, :]
+
+    sizes = [row_count] + [tail] * bool(tail)
     whole = pl.BlockSpec(memory_space=pltpu.VMEM)
     return pl.pallas_call(
         body,
-        out_shape=jax.ShapeDtypeStruct((row_count, columns), jnp.bfloat16),
-        in_specs=[pl.BlockSpec(memory_space=pltpu.SMEM)] + [whole] * 5,
+        out_shape=[jax.ShapeDtypeStruct((size, columns), jnp.bfloat16) for size in sizes],
+        in_specs=[pl.BlockSpec(memory_space=pltpu.SMEM)]
+        + [whole] * 3
+        + [pl.BlockSpec(memory_space=pltpu.HBM)],
+        out_specs=[whole] * len(sizes),
+        scratch_shapes=[
+            pltpu.VMEM(tables.shape, tables.dtype),
+            pltpu.VMEM((width, columns), jnp.bfloat16),
+            pltpu.SemaphoreType.DMA,
+        ],
+        compiler_params=pltpu.CompilerParams(vmem_limit_bytes=12 << 20),
+        cost_estimate=pl.CostEstimate(flops=0, transcendentals=0, bytes_accessed=0),
+        name="projection",
+    )(order, tokens, weight, gain.reshape(1, -1), tables)
+
+
+def passed_on(rows):
+    def body(rows_ref, out_ref):
+        out_ref[...] = rows_ref[...]
+
+    whole = pl.BlockSpec(memory_space=pltpu.VMEM)
+    return pl.pallas_call(
+        body,
+        out_shape=jax.ShapeDtypeStruct(rows.shape, rows.dtype),
+        in_specs=[whole],
         out_specs=whole,
-        scratch_shapes=[pltpu.VMEM((width, columns), jnp.bfloat16)],
-        compiler_params=pltpu.CompilerParams(vmem_limit_bytes=40 << 20),
-        cost_estimate=pl.CostEstimate(
-            flops=2 * row_count * width * columns,
-            transcendentals=0,
-            bytes_accessed=2 * width * (row_count + columns),
-        ),
-        name="projection",
-    )(core, tokens, weight, gain.reshape(1, -1), cosine, sine)
+        cost_estimate=pl.CostEstimate(flops=COST, transcendentals=0, bytes_accessed=rows.size * 4),
+        name="passed_on",
+    )(rows)
 
 
 def attention(queries, pieces, offset):
@@ -141,7 +175,7 @@
         in_specs=[pl.BlockSpec(memory_space=pltpu.SMEM)] + [whole] * (1 + len(pieces)),
         out_specs=whole,
         scratch_shapes=[pltpu.VMEM((before + row_count, 2 * head_size), jnp.bfloat16)],
-        compiler_params=pltpu.CompilerParams(vmem_limit_bytes=32 << 20),
+        compiler_params=pltpu.CompilerParams(vmem_limit_bytes=12 << 20),
         cost_estimate=pl.CostEstimate(
             flops=4 * row_count * q_width * reach,
             transcendentals=row_count * heads * reach,
@@ -156,7 +190,6 @@
     head_size = query_gain.shape[0]
     kv_width = 2 * head_size
     low = lax.axis_index("zh") == 0
-    core = lax.axis_index("core").astype(jnp.int32).reshape(1)
 
     mine = jnp.concatenate([key_weight, value_weight, w_query], axis=1)
     other = lax.ppermute(mine, "zh", [(0, 1), (1, 0)])
@@ -165,23 +198,32 @@
     )
     line = round_ring(pair, 0)
     all_kv = round_ring(line[:, :, :kv_width], 1)
-    line_q, all_kv = lax.optimization_barrier((line[:, :, kv_width:], all_kv))
-    all_q = round_ring(line_q, 1)
 
     offset = (lax.axis_index(CTX) * row_count).astype(jnp.int32)
     position = (offset + jnp.arange(row_count, dtype=jnp.int32)).astype(jnp.float32)
-    cosine, sine = rotary_tables(position, head_size)
-
-    kv = projection(tokens, all_kv, key_gain, cosine, sine, core, 1)
-    reach = WINDOW - 1
-    hop_count = (reach + row_count - 1) // row_count
-    needed = [min(row_count, reach - distance * row_count) for distance in range(hop_count)]
-    sizes = [-(-rows // 16) * 16 for rows in needed]
-    received = [
-        from_behind(kv[row_count - size :], distance + 1) for distance, size in enumerate(sizes)
-    ]
-    queries = projection(tokens, all_q, query_gain, cosine, sine, core, 2)
-    return attention(queries, received[::-1] + [kv], offset)
+    tables = rotary_tables(position, head_size)
+
+    all_kv, tables = lax.optimization_barrier((all_kv, tables))
+    line_q = line[:, :, kv_width:]
+    all_q = jnp.stack([line_q] + [along_ring(line_q, 1, shift) for shift in SHIFTS[1:]])
+
+    y = jnp.repeat(jnp.arange(SIDE, dtype=jnp.int32), SIDE)
+    x = jnp.tile(jnp.arange(SIDE, dtype=jnp.int32), SIDE)
+    first_core = lax.axis_index("core") == 0
+    outer = jnp.where(first_core, y, x)
+    inner = jnp.where(first_core, x, y)
+    here = jnp.where(first_core, lax.axis_index("y"), lax.axis_index("x"))
+    shift = (here - outer) % SIDE
+    kv_order = outer * SIDE + inner
+    q_order = jnp.where(shift == 2, 3, jnp.where(shift == 3, 2, shift)) * SIDE + inner
+
+    far_rows = -(-(WINDOW - 1 - 2 * row_count) // 16) * 16
+    kv, tail = projection(tokens, all_kv, kv_order, key_gain, tables, 1, far_rows)
+    near = from_behind(kv, 1)
+    far = from_behind(tail, 3)
+    middle = from_behind(passed_on(kv), 2)
+    (queries,) = projection(tokens, all_q, q_order, query_gain, tables, 2)
+    return attention(queries, [far, middle, near, kv], offset)
 
 
 def solution(mesh):

time: 130 us -> 122 us (0.938)
  the two profiles are of different devices: /device:TPU:112 before, /device:TPU:70 now
where the time goes in v3:
time: 122 us; the launch traced here: 121 us
  starting transfers between devices  54.6 us (45%)
  waiting for transfers between devices  25.2 us (21%)
  blocking collectives  15.2 us (12%)
  Pallas kernels  11.6 us (10%)
  local copies, waits for them, and re-layouts  10.6 us (9%)
  other arithmetic  3.73 us (3%)
    ppermute x3, starting transfers between devices, from_behind(): lax.ppermute(block, CTX, [(i - distance, i) for i in range(distance, coun...  24.9 us
    all_to_all x1, blocking collectives, round_ring(): lax.all_to_all(sent, CTX + HEAD, 0, 0, tiled=True, axis_index_groups=ring...  15.2 us
    ppermute x1, starting transfers between devices, on_device(): other = lax.ppermute(mine, 'zh', [(0, 1), (1, 0)])  13.9 us
    ppermute x1, waiting for transfers between devices, on_device(): other = lax.ppermute(mine, 'zh', [(0, 1), (1, 0)])  11.6 us
    ppermute x3, starting transfers between devices, along_ring(): return lax.ppermute(block, CTX + HEAD, pairs)  11.3 us
    ppermute x3, waiting for transfers between devices, from_behind(): lax.ppermute(block, CTX, [(i - distance, i) for i in range(distance, coun...  6.99 us
    all_to_all x1, waiting for transfers between devices, round_ring(): lax.all_to_all(sent, CTX + HEAD, 0, 0, tiled=True, axis_index_groups=ring...  6.62 us
    pallas_call x2, Pallas kernels, projection(): pl.pallas_call(body, out_shape=[jax.ShapeDtypeStruct((size, columns), jnp...  6.36 us
  transfers between devices with their start and end apart: 8, of which 3 were waited for; matrix products, arithmetic and copies ran while one was open for 3% of the time, Pallas kernels for 7%

profile of v3, /device:TPU:70, one launch (start us, length us, event | category | flops | bytes accessed | tf_op | source)
XLA Modules:
  0.0 121.1 jit_solution(7185024992960462940)
XLA Ops:
  0.0 0.8 constant_dynamic-update-slice_fusion.2
  0.8 0.8 constant_dynamic-update-slice_fusion.1
  1.6 0.9 constant_dynamic-update-slice_fusion
  2.5 13.9 %collective-permute-start = (bf16[168,512]{1,0:T(8,128)(2,1)S(1)}, bf16[168,512]{1,0:T(8,128)(2,1)S(1)}, u32[]{:S(2)}, u32[]{:S(2)}) collective-permute-start(bf16[168,512]{1,0:T(8,128)(2,1)S(1)} %constant_dynamic-update-slice_fusion), channel_id=1, source_target_pairs={{0,16},{16,0},{1,17},{17,1},{2,18},{18,2},{3,19},{19,3},{4,20},{20... | collective-permute-start | bytes 516104 | tf_op jit(solution)/shard_map/ppermute | solution.py:195
  16.4 11.6 %collective-permute-done = bf16[168,512]{1,0:T(8,128)(2,1)S(1)} collective-permute-done((bf16[168,512]{1,0:T(8,128)(2,1)S(1)}, bf16[168,512]{1,0:T(8,128)(2,1)S(1)}, u32[]{:S(2)}, u32[]{:S(2)}) %collective-permute-start) | collective-permute-done | bytes 172064 | tf_op jit(solution)/shard_map/ppermute | solution.py:195
  28.0 0.1 maximum_select_fusion
  28.1 0.1 broadcast_in_dim.24
  28.2 15.2 %all_to_all.10 = bf16[4,336,512]{2,1,0:T(8,128)(2,1)S(1)} all-to-all(bf16[4,336,512]{2,1,0:T(8,128)(2,1)S(1)} %broadcast_in_dim.24), channel_id=1, replica_groups={{0,32,64,96},{128,160,192,224},{256,288,320,352},{384,416,448,480},{1,1..., dimensions={0} | all-to-all | bytes 2752512 | tf_op jit(solution)/shard_map/all_to_all | solution.py:33
  43.4 1.2 %fusion.6 = (bf16[4,336,256]{2,1,0:T(8,128)(2,1)S(1)}, bf16[1,4,336,256]{3,2,1,0:T(8,128)(2,1)}, bf16[4,336,256]{2,1,0:T(8,128)(2,1)}) fusion(bf16[4,336,512]{2,1,0:T(8,128)(2,1)S(1)} %all_to_all.10), kind=kLoop, calls=%fused_computation.26 | loop fusion | bytes 3440640 | tf_op jit(solution)/shard_map/slice | solution.py:200
  44.6 1.7 %broadcast_in_dim.25 = bf16[4,4,336,256]{3,2,1,0:T(8,128)(2,1)} broadcast(bf16[4,336,256]{2,1,0:T(8,128)(2,1)S(1)} %get-tuple-element.13), dimensions={1,2,3} | broadcast | bytes 3440640 | tf_op jit(solution)/shard_map/broadcast_in_dim | solution.py:32
  46.3 4.5 %all-to-all-start.1 = ((bf16[4,4,336,256]{3,2,1,0:T(8,128)(2,1)}), bf16[4,4,336,256]{3,2,1,0:T(8,128)(2,1)S(1)}, u32[]{:S(2)}, u32[]{:S(2)}) async-start(bf16[4,4,336,256]{3,2,1,0:T(8,128)(2,1)} %broadcast_in_dim.25), calls=%async_computation.1 | async-start | bytes 5505024 | tf_op jit(solution)/shard_map/all_to_all | solution.py:33
  50.8 0.0 copy-start.2
  50.8 0.1 sub.11
  50.9 0.1 mul.51
  51.0 0.1 select_n.52
  51.1 0.9 multiply_cosine_fusion
  52.0 0.2 maximum_bitcast_fusion
  52.2 0.8 pad_maximum_fusion.1.tables_ref
  53.0 3.9 %collective-permute-start.1 = (bf16[4,336,256]{2,1,0:T(8,128)(2,1)}, bf16[4,336,256]{2,1,0:T(8,128)(2,1)}, u32[]{:S(2)}, u32[]{:S(2)}) collective-permute-start(bf16[4,336,256]{2,1,0:T(8,128)(2,1)} %get-tuple-element.15), channel_id=1, source_target_pairs={{384,0},{0,128},{128,256},{256,384},{416,32},{32,160},{160,288},{2... | collective-permute-start | bytes 2064392 | tf_op jit(solution)/shard_map/ppermute | solution.py:38
  56.9 3.1 %collective-permute-start.2 = (bf16[4,336,256]{2,1,0:T(8,128)(2,1)}, bf16[4,336,256]{2,1,0:T(8,128)(2,1)}, u32[]{:S(2)}, u32[]{:S(2)}) collective-permute-start(bf16[4,336,256]{2,1,0:T(8,128)(2,1)} %get-tuple-element.15), channel_id=1, source_target_pairs={{128,0},{256,128},{384,256},{0,384},{160,32},{288,160},{416,288},{... | collective-permute-start | bytes 2064392 | tf_op jit(solution)/shard_map/ppermute | solution.py:38
  60.1 4.2 %collective-permute-start.3 = (bf16[4,336,256]{2,1,0:T(8,128)(2,1)}, bf16[4,336,256]{2,1,0:T(8,128)(2,1)}, u32[]{:S(2)}, u32[]{:S(2)}) collective-permute-start(bf16[4,336,256]{2,1,0:T(8,128)(2,1)} %get-tuple-element.15), channel_id=1, source_target_pairs={{256,0},{384,128},{0,256},{128,384},{288,32},{416,160},{32,288},{1... | collective-permute-start | bytes 2064392 | tf_op jit(solution)/shard_map/ppermute | solution.py:38
  64.3 6.6 %all-to-all-done.1 = bf16[4,4,336,256]{3,2,1,0:T(8,128)(2,1)S(1)} async-done(((bf16[4,4,336,256]{3,2,1,0:T(8,128)(2,1)}), bf16[4,4,336,256]{3,2,1,0:T(8,128)(2,1)S(1)}, u32[]{:S(2)}, u32[]{:S(2)}) %all-to-all-start.1) | async-done | bytes 2752544 | tf_op jit(solution)/shard_map/all_to_all | solution.py:33
  70.9 0.0 copy-done.2
  70.9 0.0 copy-start
  70.9 2.4 %copy-done = bf16[448,5376]{1,0:T(8,128)(2,1)S(1)} copy-done((bf16[448,5376]{1,0:T(8,128)(2,1)S(1)}, bf16[448,5376]{1,0:T(8,128)(2,1)}, u32[]{:S(2)}) %copy-start) | copy-done | bytes 4816920
  73.3 3.1 %projection.3 = (bf16[448,256]{1,0:T(8,128)(2,1)S(1)}, bf16[128,256]{1,0:T(8,128)(2,1)S(1)}) custom-call(s32[16]{0:T(128)S(1)} %get-tuple-element.19.order_ref, bf16[448,5376]{1,0:T(8,128)(2,1)S(1)} %copy-done, bf16[16,336,256]{2,1,0:T(8,128)(2,1)S(1)} %bitcast.14, f32[1,128]{1,0:T(1,128)S(1)} %bitcast.16, f32[2,448,128]{2,1,0:T(8,128)} %pad_maximum_fusion.1.tables_ref), custom_call_target="tpu_custom_call" | custom-call | tf_op jit(solution)/shard_map/projection/pallas_call | solution.py:91
  76.4 0.0 copy-start.4
  76.4 0.0 copy-start.6
  76.4 15.6 %collective-permute-start.6 = (bf16[448,256]{1,0:T(8,128)(2,1)S(1)}, bf16[448,256]{1,0:T(8,128)(2,1)S(1)}, u32[]{:S(2)}, u32[]{:S(2)}) collective-permute-start(bf16[448,256]{1,0:T(8,128)(2,1)S(1)} %get-tuple-element.12.rows_ref.refs_3_), channel_id=1, source_target_pairs={{0,16},{16,32},{32,48},{48,64},{64,80},{80,96},{96,112},{112,128},... | collective-permute-start | bytes 688136 | tf_op jit(solution)/shard_map/ppermute | solution.py:43
  92.1 0.0 copy-done.4
  92.1 1.6 %passed_on.1 = bf16[448,256]{1,0:T(8,128)(2,1)} custom-call(bf16[448,256]{1,0:T(8,128)(2,1)} %copy-done.4), custom_call_target="tpu_custom_call" | custom-call | flops 10000000000 | bytes 458752 | tf_op jit(solution)/shard_map/passed_on/pallas_call | solution.py:114
  93.7 3.9 %collective-permute-start.5 = (bf16[448,256]{1,0:T(8,128)(2,1)}, bf16[448,256]{1,0:T(8,128)(2,1)S(1)}, u32[]{:S(2)}, u32[]{:S(2)}) collective-permute-start(bf16[448,256]{1,0:T(8,128)(2,1)} %passed_on.1), channel_id=1, source_target_pairs={{0,32},{16,48},{32,64},{48,80},{64,96},{80,112},{96,128},{112,144}... | collective-permute-start | bytes 688136 | tf_op jit(solution)/shard_map/ppermute | solution.py:43
  97.7 0.0 collective-permute-done.1
  97.7 5.4 %collective-permute-start.4 = (bf16[128,256]{1,0:T(8,128)(2,1)S(1)}, bf16[128,256]{1,0:T(8,128)(2,1)S(1)}, u32[]{:S(2)}, u32[]{:S(2)}) collective-permute-start(bf16[128,256]{1,0:T(8,128)(2,1)S(1)} %get-tuple-element.11), channel_id=1, source_target_pairs={{0,48},{16,64},{32,80},{48,96},{64,112},{80,128},{96,144},{112,160... | collective-permute-start | bytes 196616 | tf_op jit(solution)/shard_map/ppermute | solution.py:43
  103.1 0.0 collective-permute-done.2
  103.1 0.0 collective-permute-done.3
  103.1 0.0 copy-done.6
  103.1 0.0 copy-start.3
  103.1 1.7 %pad_maximum_fusion = bf16[4,4,336,256]{3,2,1,0:T(8,128)(2,1)S(1)} fusion(bf16[1,4,336,256]{3,2,1,0:T(8,128)(2,1)} %bitcast.4, bf16[1,4,336,256]{3,2,1,0:T(8,128)(2,1)} %bitcast.3, bf16[1,4,336,256]{3,2,1,0:T(8,128)(2,1)} %bitcast.2, bf16[1,4,336,256]{3,2,1,0:T(8,128)(2,1)S(1)} %copy-done.6), kind=kLoop, calls=%fused_computation | loop fusion | flops 4128768 | bytes 5505024 | tf_op jit(solution)/shard_map/stack | solution.py:208
  104.8 0.0 copy-done.3
  104.8 0.0 copy-start.1
  104.8 2.4 %copy-done.1 = bf16[448,5376]{1,0:T(8,128)(2,1)S(1)} copy-done((bf16[448,5376]{1,0:T(8,128)(2,1)S(1)}, bf16[448,5376]{1,0:T(8,128)(2,1)}, u32[]{:S(2)}) %copy-start.1) | copy-done | bytes 4816920
  107.2 3.3 %projection.2.queries_ref = bf16[448,256]{1,0:T(8,128)(2,1)S(1)} custom-call(s32[16]{0:T(128)S(1)} %get-tuple-element.20.order_ref, bf16[448,5376]{1,0:T(8,128)(2,1)S(1)} %copy-done.1, bf16[16,336,256]{2,1,0:T(8,128)(2,1)S(1)} %bitcast.15, f32[1,128]{1,0:T(1,128)S(1)} %bitcast.17, f32[2,448,128]{2,1,0:T(8,128)} %pad_maximum_fusion.1.tables_ref), custom_call_target="tpu_custom_call" | custom-call | tf_op jit(solution)/shard_map/projection/pallas_call | solution.py:91
  110.5 7.0 %collective-permute-done.4.refs_0_ = bf16[128,256]{1,0:T(8,128)(2,1)S(1)} collective-permute-done((bf16[128,256]{1,0:T(8,128)(2,1)S(1)}, bf16[128,256]{1,0:T(8,128)(2,1)S(1)}, u32[]{:S(2)}, u32[]{:S(2)}) %collective-permute-start.4) | collective-permute-done | bytes 65568 | tf_op jit(solution)/shard_map/ppermute | solution.py:43
  117.4 0.0 collective-permute-done.5.refs_1_
  117.4 0.0 collective-permute-done.6.refs_2_
  117.4 0.0 copy-done.5
  117.5 3.6 %attention.1 = bf16[448,256]{1,0:T(8,128)(2,1)} custom-call(s32[1]{0:T(128)} %bitcast.offset_ref, bf16[448,256]{1,0:T(8,128)(2,1)S(1)} %projection.2.queries_ref, bf16[128,256]{1,0:T(8,128)(2,1)S(1)} %collective-permute-done.4.refs_0_, bf16[448,256]{1,0:T(8,128)(2,1)S(1)} %collective-permute-done.5.refs_1_, ...), custom_call_target="tpu_custom_call" | custom-call | flops 499122176 | bytes 1212416 | tf_op jit(solution)/shard_map/attention/pallas_call | solution.py:172
  (6 shorter events, 0.0 us)
Async XLA Ops:
  2.5 25.5 %collective-permute-start = (bf16[168,512]{1,0:T(8,128)(2,1)S(1)}, bf16[168,512]{1,0:T(8,128)(2,1)S(1)}, u32[]{:S(2)}, u32[]{:S(2)}) collective-permute-start(bf16[168,512]{1,0:T(8,128)(2,1)S(1)} %constant_dynamic-update-slice_fusion), channel_id=1, source_target_pairs={{0,16},{16,0},{1,17},{17,1},{2,18},{18,2},{3,19},{19,3},{4,20},{20... | collective-permute-start | bytes 516104 | tf_op jit(solution)/shard_map/ppermute | solution.py:195
  46.3 24.6 %all-to-all-start.1 = ((bf16[4,4,336,256]{3,2,1,0:T(8,128)(2,1)}), bf16[4,4,336,256]{3,2,1,0:T(8,128)(2,1)S(1)}, u32[]{:S(2)}, u32[]{:S(2)}) async-start(bf16[4,4,336,256]{3,2,1,0:T(8,128)(2,1)} %broadcast_in_dim.25), calls=%async_computation.1 | async-start | bytes 5505024 | tf_op jit(solution)/shard_map/all_to_all | solution.py:33
  50.8 20.1 %copy-start.2 = (f32[128]{0:T(128)S(1)}, f32[128]{0:T(128)}, u32[]{:S(2)}) copy-start(f32[128]{0:T(128)} %param.11) | copy-start | bytes 1540
  53.0 44.7 %collective-permute-start.1 = (bf16[4,336,256]{2,1,0:T(8,128)(2,1)}, bf16[4,336,256]{2,1,0:T(8,128)(2,1)}, u32[]{:S(2)}, u32[]{:S(2)}) collective-permute-start(bf16[4,336,256]{2,1,0:T(8,128)(2,1)} %get-tuple-element.15), channel_id=1, source_target_pairs={{384,0},{0,128},{128,256},{256,384},{416,32},{32,160},{160,288},{2... | collective-permute-start | bytes 2064392 | tf_op jit(solution)/shard_map/ppermute | solution.py:38
  56.9 46.1 %collective-permute-start.2 = (bf16[4,336,256]{2,1,0:T(8,128)(2,1)}, bf16[4,336,256]{2,1,0:T(8,128)(2,1)}, u32[]{:S(2)}, u32[]{:S(2)}) collective-permute-start(bf16[4,336,256]{2,1,0:T(8,128)(2,1)} %get-tuple-element.15), channel_id=1, source_target_pairs={{128,0},{256,128},{384,256},{0,384},{160,32},{288,160},{416,288},{... | collective-permute-start | bytes 2064392 | tf_op jit(solution)/shard_map/ppermute | solution.py:38
  60.1 43.0 %collective-permute-start.3 = (bf16[4,336,256]{2,1,0:T(8,128)(2,1)}, bf16[4,336,256]{2,1,0:T(8,128)(2,1)}, u32[]{:S(2)}, u32[]{:S(2)}) collective-permute-start(bf16[4,336,256]{2,1,0:T(8,128)(2,1)} %get-tuple-element.15), channel_id=1, source_target_pairs={{256,0},{384,128},{0,256},{128,384},{288,32},{416,160},{32,288},{1... | collective-permute-start | bytes 2064392 | tf_op jit(solution)/shard_map/ppermute | solution.py:38
  70.9 2.4 %copy-start = (bf16[448,5376]{1,0:T(8,128)(2,1)S(1)}, bf16[448,5376]{1,0:T(8,128)(2,1)}, u32[]{:S(2)}) copy-start(bf16[448,5376]{1,0:T(8,128)(2,1)} %tokens_ref.3) | copy-start | bytes 14450692
  76.4 15.7 %copy-start.4 = (bf16[448,256]{1,0:T(8,128)(2,1)}, bf16[448,256]{1,0:T(8,128)(2,1)S(1)}, u32[]{:S(2)}) copy-start(bf16[448,256]{1,0:T(8,128)(2,1)S(1)} %get-tuple-element.12.rows_ref.refs_3_) | copy-start | bytes 688132
  76.4 26.7 %copy-start.6 = (bf16[1,4,336,256]{3,2,1,0:T(8,128)(2,1)S(1)}, bf16[1,4,336,256]{3,2,1,0:T(8,128)(2,1)}, u32[]{:S(2)}) copy-start(bf16[1,4,336,256]{3,2,1,0:T(8,128)(2,1)} %get-tuple-element.14) | copy-start | bytes 2064388
  76.4 41.0 %collective-permute-start.6 = (bf16[448,256]{1,0:T(8,128)(2,1)S(1)}, bf16[448,256]{1,0:T(8,128)(2,1)S(1)}, u32[]{:S(2)}, u32[]{:S(2)}) collective-permute-start(bf16[448,256]{1,0:T(8,128)(2,1)S(1)} %get-tuple-element.12.rows_ref.refs_3_), channel_id=1, source_target_pairs={{0,16},{16,32},{32,48},{48,64},{64,80},{80,96},{96,112},{112,128},... | collective-permute-start | bytes 688136 | tf_op jit(solution)/shard_map/ppermute | solution.py:43
  93.7 23.7 %collective-permute-start.5 = (bf16[448,256]{1,0:T(8,128)(2,1)}, bf16[448,256]{1,0:T(8,128)(2,1)S(1)}, u32[]{:S(2)}, u32[]{:S(2)}) collective-permute-start(bf16[448,256]{1,0:T(8,128)(2,1)} %passed_on.1), channel_id=1, source_target_pairs={{0,32},{16,48},{32,64},{48,80},{64,96},{80,112},{96,128},{112,144}... | collective-permute-start | bytes 688136 | tf_op jit(solution)/shard_map/ppermute | solution.py:43
  97.7 19.8 %collective-permute-start.4 = (bf16[128,256]{1,0:T(8,128)(2,1)S(1)}, bf16[128,256]{1,0:T(8,128)(2,1)S(1)}, u32[]{:S(2)}, u32[]{:S(2)}) collective-permute-start(bf16[128,256]{1,0:T(8,128)(2,1)S(1)} %get-tuple-element.11), channel_id=1, source_target_pairs={{0,48},{16,64},{32,80},{48,96},{64,112},{80,128},{96,144},{112,160... | collective-permute-start | bytes 196616 | tf_op jit(solution)/shard_map/ppermute | solution.py:43
  103.1 1.7 %copy-start.3 = (f32[128]{0:T(128)S(1)}, f32[128]{0:T(128)}, u32[]{:S(2)}) copy-start(f32[128]{0:T(128)} %param.10) | copy-start | bytes 1540
  104.8 2.4 %copy-start.1 = (bf16[448,5376]{1,0:T(8,128)(2,1)S(1)}, bf16[448,5376]{1,0:T(8,128)(2,1)}, u32[]{:S(2)}) copy-start(bf16[448,5376]{1,0:T(8,128)(2,1)} %tokens_ref.3) | copy-start | bytes 14450692
  107.2 10.3 %copy-start.5 = (bf16[448,256]{1,0:T(8,128)(2,1)S(1)}, bf16[448,256]{1,0:T(8,128)(2,1)}, u32[]{:S(2)}) copy-start(bf16[448,256]{1,0:T(8,128)(2,1)} %copy-done.4) | copy-start | bytes 688132

commit v4 on v3

--- a/solution.py
+++ b/solution.py
@@ -14,7 +14,7 @@
 CTX = ("y", "x", "zh")
 HEAD = ("zl", "core")
 QUERY_BLOCK = 64
-COST = 10**10
+OPERANDS = (0, 2, 1, 3)
 
 query_scale = 168.0 ** (-0.5)
 
@@ -53,6 +53,25 @@
     return jnp.stack(
         [jnp.concatenate([cosine, cosine], 1), jnp.concatenate([-sine, sine], 1)]
     )
+
+
+def side_by_side(*arrays):
+    widths = [array.shape[1] for array in arrays]
+
+    def body(*refs):
+        start = 0
+        for ref, width in zip(refs, widths):
+            refs[-1][:, start : start + width] = ref[...]
+            start += width
+
+    whole = pl.BlockSpec(memory_space=pltpu.VMEM)
+    return pl.pallas_call(
+        body,
+        out_shape=jax.ShapeDtypeStruct((arrays[0].shape[0], sum(widths)), arrays[0].dtype),
+        in_specs=[whole] * len(arrays),
+        out_specs=whole,
+        name="side_by_side",
+    )(*arrays)
 
 
 def projection(tokens, weight, order, gain, tables, normed_heads, tail=0):
@@ -106,35 +125,19 @@
     )(order, tokens, weight, gain.reshape(1, -1), tables)
 
 
-def passed_on(rows):
-    def body(rows_ref, out_ref):
-        out_ref[...] = rows_ref[...]
-
-    whole = pl.BlockSpec(memory_space=pltpu.VMEM)
-    return pl.pallas_call(
-        body,
-        out_shape=jax.ShapeDtypeStruct(rows.shape, rows.dtype),
-        in_specs=[whole],
-        out_specs=whole,
-        cost_estimate=pl.CostEstimate(flops=COST, transcendentals=0, bytes_accessed=rows.size * 4),
-        name="passed_on",
-    )(rows)
-
-
 def attention(queries, pieces, offset):
     row_count, q_width = queries.shape
     head_size = pieces[0].shape[1] // 2
     heads = q_width // head_size
     sizes = [piece.shape[0] for piece in pieces]
     before = sum(sizes[:-1])
+    starts = [sum(sizes[:i]) for i in range(len(sizes))]
     reach = before + QUERY_BLOCK
 
     def body(offset_ref, queries_ref, *refs):
         piece_refs, out_ref, all_ref = refs[:-2], refs[-2], refs[-1]
-        start = 0
-        for piece_ref, size in zip(piece_refs, sizes):
-            all_ref[start : start + size, :] = piece_ref[...]
-            start += size
+        for piece_ref, i in zip(piece_refs, OPERANDS):
+            all_ref[starts[i] : starts[i] + sizes[i], :] = piece_ref[...]
         shape = (heads, QUERY_BLOCK, reach)
         row = lax.broadcasted_iota(jnp.int32, shape, 1).reshape(heads * QUERY_BLOCK, reach)
         column = lax.broadcasted_iota(jnp.int32, shape, 2).reshape(heads * QUERY_BLOCK, reach)
@@ -182,7 +185,7 @@
             bytes_accessed=4 * (row_count * q_width + (before + row_count) * head_size),
         ),
         name="attention",
-    )(offset.reshape(1), queries, *pieces)
+    )(offset.reshape(1), queries, *[pieces[i] for i in OPERANDS])
 
 
 def on_device(tokens, w_query, key_weight, value_weight, query_gain, key_gain):
@@ -191,7 +194,7 @@
     kv_width = 2 * head_size
     low = lax.axis_index("zh") == 0
 
-    mine = jnp.concatenate([key_weight, value_weight, w_query], axis=1)
+    mine = side_by_side(key_weight, value_weight, w_query)
     other = lax.ppermute(mine, "zh", [(0, 1), (1, 0)])
     pair = jnp.where(
         low, jnp.concatenate([mine, other], axis=0), jnp.concatenate([other, mine], axis=0)
@@ -221,7 +224,7 @@
     kv, tail = projection(tokens, all_kv, kv_order, key_gain, tables, 1, far_rows)
     near = from_behind(kv, 1)
     far = from_behind(tail, 3)
-    middle = from_behind(passed_on(kv), 2)
+    middle = from_behind(kv, 2)
     (queries,) = projection(tokens, all_q, q_order, query_gain, tables, 2)
     return attention(queries, [far, middle, near, kv], offset)
 

time: 122 us -> 121 us (level)
  the two profiles are of different devices: /device:TPU:70 before, /device:TPU:74 now
where the time goes in v4:
time: 121 us; the launch traced here: 120 us
  starting transfers between devices  50.7 us (42%)
  waiting for transfers between devices  31.3 us (26%)
  blocking collectives  15.8 us (13%)
  Pallas kernels  11.6 us (10%)
  local copies, waits for them, and re-layouts  5.73 us (5%)
  other arithmetic  4.71 us (4%)
    ppermute x3, starting transfers between devices, from_behind(): lax.ppermute(block, CTX, [(i - distance, i) for i in range(distance, coun...  22 us
    all_to_all x1, blocking collectives, round_ring(): lax.all_to_all(sent, CTX + HEAD, 0, 0, tiled=True, axis_index_groups=ring...  15.8 us
    ppermute x1, starting transfers between devices, on_device(): other = lax.ppermute(mine, 'zh', [(0, 1), (1, 0)])  13.9 us
    ppermute x3, waiting for transfers between devices, from_behind(): lax.ppermute(block, CTX, [(i - distance, i) for i in range(distance, coun...  12.9 us
    ppermute x1, waiting for transfers between devices, on_device(): other = lax.ppermute(mine, 'zh', [(0, 1), (1, 0)])  11.8 us
    ppermute x3, starting transfers between devices, along_ring(): return lax.ppermute(block, CTX + HEAD, pairs)  9.82 us
    all_to_all x1, waiting for transfers between devices, round_ring(): lax.all_to_all(sent, CTX + HEAD, 0, 0, tiled=True, axis_index_groups=ring...  6.62 us
    pallas_call x2, Pallas kernels, projection(): pl.pallas_call(body, out_shape=[jax.ShapeDtypeStruct((size, columns), jnp...  6.36 us
  transfers between devices with their start and end apart: 8, of which 3 were waited for; matrix products, arithmetic and copies ran while one was open for 3% of the time, Pallas kernels for 5%

profile of v4, /device:TPU:74, one launch (start us, length us, event | category | flops | bytes accessed | tf_op | source)
XLA Modules:
  0.0 120.1 jit_solution(13744701260138442532)
XLA Ops:
  0.0 1.6 %side_by_side.1 = bf16[168,512]{1,0:T(8,128)(2,1)} custom-call(bf16[168,128]{1,0:T(8,128)(2,1)} %refs_0_.1, bf16[168,128]{1,0:T(8,128)(2,1)} %refs_1_.1, bf16[168,256]{1,0:T(8,128)(2,1)} %refs_2_.1), custom_call_target="tpu_custom_call" | custom-call | tf_op jit(solution)/shard_map/side_by_side/pallas_call | solution.py:68
  1.6 13.9 %collective-permute-start = (bf16[168,512]{1,0:T(8,128)(2,1)}, bf16[168,512]{1,0:T(8,128)(2,1)S(1)}, u32[]{:S(2)}, u32[]{:S(2)}) collective-permute-start(bf16[168,512]{1,0:T(8,128)(2,1)} %side_by_side.1), channel_id=1, source_target_pairs={{0,16},{16,0},{1,17},{17,1},{2,18},{18,2},{3,19},{19,3},{4,20},{20... | collective-permute-start | bytes 516104 | tf_op jit(solution)/shard_map/ppermute | solution.py:198
  15.6 11.8 %collective-permute-done = bf16[168,512]{1,0:T(8,128)(2,1)S(1)} collective-permute-done((bf16[168,512]{1,0:T(8,128)(2,1)}, bf16[168,512]{1,0:T(8,128)(2,1)S(1)}, u32[]{:S(2)}, u32[]{:S(2)}) %collective-permute-start) | collective-permute-done | bytes 172064 | tf_op jit(solution)/shard_map/ppermute | solution.py:198
  27.3 1.1 maximum_select_fusion
  28.4 0.1 broadcast_in_dim.24
  28.6 15.8 %all_to_all.10 = bf16[4,336,512]{2,1,0:T(8,128)(2,1)S(1)} all-to-all(bf16[4,336,512]{2,1,0:T(8,128)(2,1)S(1)} %broadcast_in_dim.24), channel_id=1, replica_groups={{0,32,64,96},{128,160,192,224},{256,288,320,352},{384,416,448,480},{1,1..., dimensions={0} | all-to-all | bytes 2752512 | tf_op jit(solution)/shard_map/all_to_all | solution.py:33
  44.4 1.3 %fusion.6 = (bf16[4,336,256]{2,1,0:T(8,128)(2,1)S(1)}, bf16[1,4,336,256]{3,2,1,0:T(8,128)(2,1)}, bf16[4,336,256]{2,1,0:T(8,128)(2,1)}) fusion(bf16[4,336,512]{2,1,0:T(8,128)(2,1)S(1)} %all_to_all.10), kind=kLoop, calls=%fused_computation.23 | loop fusion | bytes 3440640 | tf_op jit(solution)/shard_map/slice | solution.py:203
  45.6 1.7 %broadcast_in_dim.25 = bf16[4,4,336,256]{3,2,1,0:T(8,128)(2,1)} broadcast(bf16[4,336,256]{2,1,0:T(8,128)(2,1)S(1)} %get-tuple-element.13), dimensions={1,2,3} | broadcast | bytes 3440640 | tf_op jit(solution)/shard_map/broadcast_in_dim | solution.py:32
  47.4 4.9 %all-to-all-start.1 = ((bf16[4,4,336,256]{3,2,1,0:T(8,128)(2,1)}), bf16[4,4,336,256]{3,2,1,0:T(8,128)(2,1)S(1)}, u32[]{:S(2)}, u32[]{:S(2)}) async-start(bf16[4,4,336,256]{3,2,1,0:T(8,128)(2,1)} %broadcast_in_dim.25), calls=%async_computation.1 | async-start | bytes 5505024 | tf_op jit(solution)/shard_map/all_to_all | solution.py:33
  52.3 0.0 copy-start.1
  52.3 0.1 sub.11
  52.4 0.1 mul.51
  52.4 0.1 select_n.52
  52.6 3.4 %collective-permute-start.1 = (bf16[4,336,256]{2,1,0:T(8,128)(2,1)}, bf16[4,336,256]{2,1,0:T(8,128)(2,1)}, u32[]{:S(2)}, u32[]{:S(2)}) collective-permute-start(bf16[4,336,256]{2,1,0:T(8,128)(2,1)} %get-tuple-element.15), channel_id=1, source_target_pairs={{384,0},{0,128},{128,256},{256,384},{416,32},{32,160},{160,288},{2... | collective-permute-start | bytes 2064392 | tf_op jit(solution)/shard_map/ppermute | solution.py:38
  55.9 2.5 %collective-permute-start.2 = (bf16[4,336,256]{2,1,0:T(8,128)(2,1)}, bf16[4,336,256]{2,1,0:T(8,128)(2,1)}, u32[]{:S(2)}, u32[]{:S(2)}) collective-permute-start(bf16[4,336,256]{2,1,0:T(8,128)(2,1)} %get-tuple-element.15), channel_id=1, source_target_pairs={{128,0},{256,128},{384,256},{0,384},{160,32},{288,160},{416,288},{... | collective-permute-start | bytes 2064392 | tf_op jit(solution)/shard_map/ppermute | solution.py:38
  58.4 4.0 %collective-permute-start.3 = (bf16[4,336,256]{2,1,0:T(8,128)(2,1)}, bf16[4,336,256]{2,1,0:T(8,128)(2,1)}, u32[]{:S(2)}, u32[]{:S(2)}) collective-permute-start(bf16[4,336,256]{2,1,0:T(8,128)(2,1)} %get-tuple-element.15), channel_id=1, source_target_pairs={{256,0},{384,128},{0,256},{128,384},{288,32},{416,160},{32,288},{1... | collective-permute-start | bytes 2064392 | tf_op jit(solution)/shard_map/ppermute | solution.py:38
  62.4 0.9 multiply_cosine_fusion
  63.3 0.0 slice-start
  63.3 0.2 maximum_bitcast_fusion
  63.5 0.8 pad_maximum_fusion.1.tables_ref
  64.3 6.6 %all-to-all-done.1 = bf16[4,4,336,256]{3,2,1,0:T(8,128)(2,1)S(1)} async-done(((bf16[4,4,336,256]{3,2,1,0:T(8,128)(2,1)}), bf16[4,4,336,256]{3,2,1,0:T(8,128)(2,1)S(1)}, u32[]{:S(2)}, u32[]{:S(2)}) %all-to-all-start.1) | async-done | bytes 2752544 | tf_op jit(solution)/shard_map/all_to_all | solution.py:33
  70.9 0.0 copy-done.1
  70.9 0.0 copy-start
  70.9 2.4 %copy-done = bf16[448,5376]{1,0:T(8,128)(2,1)S(1)} copy-done((bf16[448,5376]{1,0:T(8,128)(2,1)S(1)}, bf16[448,5376]{1,0:T(8,128)(2,1)}, u32[]{:S(2)}) %copy-start) | copy-done | bytes 4816920
  73.3 0.0 copy-start.3
  73.3 0.0 slice-start.1
  73.3 3.1 %projection.3 = (bf16[448,256]{1,0:T(8,128)(2,1)S(1)}, bf16[128,256]{1,0:T(8,128)(2,1)S(1)}) custom-call(s32[16]{0:T(128)S(1)} %get-tuple-element.19.order_ref, bf16[448,5376]{1,0:T(8,128)(2,1)S(1)} %copy-done, bf16[16,336,256]{2,1,0:T(8,128)(2,1)S(1)} %bitcast.16, f32[1,128]{1,0:T(1,128)S(1)} %bitcast.18, f32[2,448,128]{2,1,0:T(8,128)} %pad_maximum_fusion.1.tables_ref), custom_call_target="tpu_custom_call" | custom-call | tf_op jit(solution)/shard_map/projection/pallas_call | solution.py:110
  76.4 15.5 %collective-permute-start.5 = (bf16[448,256]{1,0:T(8,128)(2,1)S(1)}, bf16[448,256]{1,0:T(8,128)(2,1)S(1)}, u32[]{:S(2)}, u32[]{:S(2)}) collective-permute-start(bf16[448,256]{1,0:T(8,128)(2,1)S(1)} %get-tuple-element.12.refs_3_), channel_id=1, source_target_pairs={{0,16},{16,32},{32,48},{48,64},{64,80},{80,96},{96,112},{112,128},... | collective-permute-start | bytes 688136 | tf_op jit(solution)/shard_map/ppermute | solution.py:43
  91.9 2.3 %collective-permute-start.6 = (bf16[448,256]{1,0:T(8,128)(2,1)S(1)}, bf16[448,256]{1,0:T(8,128)(2,1)S(1)}, u32[]{:S(2)}, u32[]{:S(2)}) collective-permute-start(bf16[448,256]{1,0:T(8,128)(2,1)S(1)} %get-tuple-element.12.refs_3_), channel_id=1, source_target_pairs={{0,32},{16,48},{32,64},{48,80},{64,96},{80,112},{96,128},{112,144}... | collective-permute-start | bytes 688136 | tf_op jit(solution)/shard_map/ppermute | solution.py:43
  94.2 0.0 collective-permute-done.1
  94.2 4.3 %collective-permute-start.4 = (bf16[128,256]{1,0:T(8,128)(2,1)S(1)}, bf16[128,256]{1,0:T(8,128)(2,1)S(1)}, u32[]{:S(2)}, u32[]{:S(2)}) collective-permute-start(bf16[128,256]{1,0:T(8,128)(2,1)S(1)} %get-tuple-element.11), channel_id=1, source_target_pairs={{0,48},{16,64},{32,80},{48,96},{64,112},{80,128},{96,144},{112,160... | collective-permute-start | bytes 196616 | tf_op jit(solution)/shard_map/ppermute | solution.py:43
  98.5 0.0 collective-permute-done.2
  98.5 0.0 collective-permute-done.3
  98.5 0.0 copy-done.3
  98.5 0.0 copy-start.2
  98.5 1.7 %pad_maximum_fusion = bf16[4,4,336,256]{3,2,1,0:T(8,128)(2,1)S(1)} fusion(bf16[1,4,336,256]{3,2,1,0:T(8,128)(2,1)} %bitcast.4, bf16[1,4,336,256]{3,2,1,0:T(8,128)(2,1)} %bitcast.3, bf16[1,4,336,256]{3,2,1,0:T(8,128)(2,1)} %bitcast.2, bf16[1,4,336,256]{3,2,1,0:T(8,128)(2,1)S(1)} %copy-done.3), kind=kLoop, calls=%fused_computation | loop fusion | flops 4128768 | bytes 5505024 | tf_op jit(solution)/shard_map/stack | solution.py:211
  100.2 0.0 slice-done
  100.2 0.0 slice-done.1
  100.2 0.0 copy-done.2
  100.3 3.3 %projection.2.queries_ref = bf16[448,256]{1,0:T(8,128)(2,1)S(1)} custom-call(s32[16]{0:T(128)S(1)} %get-tuple-element.20.order_ref, bf16[448,5376]{1,0:T(8,128)(2,1)S(1)} %bitcast.15, bf16[16,336,256]{2,1,0:T(8,128)(2,1)S(1)} %bitcast.17, f32[1,128]{1,0:T(1,128)S(1)} %bitcast.19, f32[2,448,128]{2,1,0:T(8,128)} %pad_maximum_fusion.1.tables_ref), custom_call_target="tpu_custom_call" | custom-call | tf_op jit(solution)/shard_map/projection/pallas_call | solution.py:110
  103.5 12.9 %collective-permute-done.4.refs_0_ = bf16[128,256]{1,0:T(8,128)(2,1)S(1)} collective-permute-done((bf16[128,256]{1,0:T(8,128)(2,1)S(1)}, bf16[128,256]{1,0:T(8,128)(2,1)S(1)}, u32[]{:S(2)}, u32[]{:S(2)}) %collective-permute-start.4) | collective-permute-done | bytes 65568 | tf_op jit(solution)/shard_map/ppermute | solution.py:43
  116.5 0.0 collective-permute-done.5.refs_1_
  116.5 0.0 collective-permute-done.6.refs_2_
  116.5 3.6 %attention.1 = bf16[448,256]{1,0:T(8,128)(2,1)} custom-call(s32[1]{0:T(128)} %bitcast.offset_ref, bf16[448,256]{1,0:T(8,128)(2,1)S(1)} %projection.2.queries_ref, bf16[128,256]{1,0:T(8,128)(2,1)S(1)} %collective-permute-done.4.refs_0_, bf16[448,256]{1,0:T(8,128)(2,1)S(1)} %collective-permute-done.5.refs_1_, ...), custom_call_target="tpu_custom_call" | custom-call | flops 499122176 | bytes 1212416 | tf_op jit(solution)/shard_map/attention/pallas_call | solution.py:175
  (6 shorter events, 0.0 us)
Async XLA Ops:
  1.6 25.7 %collective-permute-start = (bf16[168,512]{1,0:T(8,128)(2,1)}, bf16[168,512]{1,0:T(8,128)(2,1)S(1)}, u32[]{:S(2)}, u32[]{:S(2)}) collective-permute-start(bf16[168,512]{1,0:T(8,128)(2,1)} %side_by_side.1), channel_id=1, source_target_pairs={{0,16},{16,0},{1,17},{17,1},{2,18},{18,2},{3,19},{19,3},{4,20},{20... | collective-permute-start | bytes 516104 | tf_op jit(solution)/shard_map/ppermute | solution.py:198
  47.4 23.6 %all-to-all-start.1 = ((bf16[4,4,336,256]{3,2,1,0:T(8,128)(2,1)}), bf16[4,4,336,256]{3,2,1,0:T(8,128)(2,1)S(1)}, u32[]{:S(2)}, u32[]{:S(2)}) async-start(bf16[4,4,336,256]{3,2,1,0:T(8,128)(2,1)} %broadcast_in_dim.25), calls=%async_computation.1 | async-start | bytes 5505024 | tf_op jit(solution)/shard_map/all_to_all | solution.py:33
  52.3 18.7 %copy-start.1 = (f32[128]{0:T(128)S(1)}, f32[128]{0:T(128)}, u32[]{:S(2)}) copy-start(f32[128]{0:T(128)} %param.11) | copy-start | bytes 1540
  52.6 41.7 %collective-permute-start.1 = (bf16[4,336,256]{2,1,0:T(8,128)(2,1)}, bf16[4,336,256]{2,1,0:T(8,128)(2,1)}, u32[]{:S(2)}, u32[]{:S(2)}) collective-permute-start(bf16[4,336,256]{2,1,0:T(8,128)(2,1)} %get-tuple-element.15), channel_id=1, source_target_pairs={{384,0},{0,128},{128,256},{256,384},{416,32},{32,160},{160,288},{2... | collective-permute-start | bytes 2064392 | tf_op jit(solution)/shard_map/ppermute | solution.py:38
  55.9 42.5 %collective-permute-start.2 = (bf16[4,336,256]{2,1,0:T(8,128)(2,1)}, bf16[4,336,256]{2,1,0:T(8,128)(2,1)}, u32[]{:S(2)}, u32[]{:S(2)}) collective-permute-start(bf16[4,336,256]{2,1,0:T(8,128)(2,1)} %get-tuple-element.15), channel_id=1, source_target_pairs={{128,0},{256,128},{384,256},{0,384},{160,32},{288,160},{416,288},{... | collective-permute-start | bytes 2064392 | tf_op jit(solution)/shard_map/ppermute | solution.py:38
  58.4 40.1 %collective-permute-start.3 = (bf16[4,336,256]{2,1,0:T(8,128)(2,1)}, bf16[4,336,256]{2,1,0:T(8,128)(2,1)}, u32[]{:S(2)}, u32[]{:S(2)}) collective-permute-start(bf16[4,336,256]{2,1,0:T(8,128)(2,1)} %get-tuple-element.15), channel_id=1, source_target_pairs={{256,0},{384,128},{0,256},{128,384},{288,32},{416,160},{32,288},{1... | collective-permute-start | bytes 2064392 | tf_op jit(solution)/shard_map/ppermute | solution.py:38
  63.3 36.9 %slice-start = ((s8[4816896]{0:T(1024)(128)(4,1)}), s8[622592]{0:T(1024)(128)(4,1)S(1)}, s32[]{:S(2)}) async-start(s8[4816896]{0:T(1024)(128)(4,1)} %bitcast.14), calls=%async_computation.2 | async-start | bytes 1245184
  70.9 2.4 %copy-start = (bf16[448,5376]{1,0:T(8,128)(2,1)S(1)}, bf16[448,5376]{1,0:T(8,128)(2,1)}, u32[]{:S(2)}) copy-start(bf16[448,5376]{1,0:T(8,128)(2,1)} %tokens_ref.3) | copy-start | bytes 14450692
  73.3 25.2 %copy-start.3 = (bf16[1,4,336,256]{3,2,1,0:T(8,128)(2,1)S(1)}, bf16[1,4,336,256]{3,2,1,0:T(8,128)(2,1)}, u32[]{:S(2)}) copy-start(bf16[1,4,336,256]{3,2,1,0:T(8,128)(2,1)} %get-tuple-element.14) | copy-start | bytes 2064388
  73.3 26.9 %slice-start.1 = ((s8[4816896]{0:T(1024)(128)(4,1)}), s8[4194304]{0:T(1024)(128)(4,1)S(1)}, s32[]{:S(2)}) async-start(s8[4816896]{0:T(1024)(128)(4,1)} %bitcast.14), calls=%async_computation.3 | async-start | bytes 8388608
  76.4 40.0 %collective-permute-start.5 = (bf16[448,256]{1,0:T(8,128)(2,1)S(1)}, bf16[448,256]{1,0:T(8,128)(2,1)S(1)}, u32[]{:S(2)}, u32[]{:S(2)}) collective-permute-start(bf16[448,256]{1,0:T(8,128)(2,1)S(1)} %get-tuple-element.12.refs_3_), channel_id=1, source_target_pairs={{0,16},{16,32},{32,48},{48,64},{64,80},{80,96},{96,112},{112,128},... | collective-permute-start | bytes 688136 | tf_op jit(solution)/shard_map/ppermute | solution.py:43
  91.9 24.6 %collective-permute-start.6 = (bf16[448,256]{1,0:T(8,128)(2,1)S(1)}, bf16[448,256]{1,0:T(8,128)(2,1)S(1)}, u32[]{:S(2)}, u32[]{:S(2)}) collective-permute-start(bf16[448,256]{1,0:T(8,128)(2,1)S(1)} %get-tuple-element.12.refs_3_), channel_id=1, source_target_pairs={{0,32},{16,48},{32,64},{48,80},{64,96},{80,112},{96,128},{112,144}... | collective-permute-start | bytes 688136 | tf_op jit(solution)/shard_map/ppermute | solution.py:43
  94.2 22.2 %collective-permute-start.4 = (bf16[128,256]{1,0:T(8,128)(2,1)S(1)}, bf16[128,256]{1,0:T(8,128)(2,1)S(1)}, u32[]{:S(2)}, u32[]{:S(2)}) collective-permute-start(bf16[128,256]{1,0:T(8,128)(2,1)S(1)} %get-tuple-element.11), channel_id=1, source_target_pairs={{0,48},{16,64},{32,80},{48,96},{64,112},{80,128},{96,144},{112,160... | collective-permute-start | bytes 196616 | tf_op jit(solution)/shard_map/ppermute | solution.py:43
  98.5 1.7 %copy-start.2 = (f32[128]{0:T(128)S(1)}, f32[128]{0:T(128)}, u32[]{:S(2)}) copy-start(f32[128]{0:T(128)} %param.10) | copy-start | bytes 1540

commit v5 on v4

--- a/solution.py
+++ b/solution.py
@@ -15,6 +15,8 @@
 HEAD = ("zl", "core")
 QUERY_BLOCK = 64
 OPERANDS = (0, 2, 1, 3)
+
+LOG2_E = 1.4426950408889634
 
 query_scale = 168.0 ** (-0.5)
 
@@ -158,9 +160,9 @@
                 block, keys, (((1,), (1,)), ((), ())), preferred_element_type=jnp.float32
             )
             allowed = in_window & (column >= before - first - offset_ref[0])
-            scores = jnp.where(allowed, scores * query_scale, jnp.float32(-1e30))
+            scores = jnp.where(allowed, scores, jnp.float32(-1e30))
             top = jnp.max(scores, axis=-1, keepdims=True)
-            weights = jnp.exp(scores - top)
+            weights = jnp.exp2((scores - top) * (query_scale * LOG2_E))
             total = jnp.sum(weights, axis=-1, keepdims=True)
             mixed = jnp.dot(
                 weights.astype(jnp.bfloat16), values, preferred_element_type=jnp.float32

time: 121 us -> 121 us (level)
  no operation moved by 1% of the time
where the time goes in v5:
time: 121 us; the launch traced here: 120 us
  starting transfers between devices  50.7 us (42%)
  waiting for transfers between devices  31.3 us (26%)
  blocking collectives  15.8 us (13%)
  Pallas kernels  11.6 us (10%)
  local copies, waits for them, and re-layouts  5.73 us (5%)
  other arithmetic  4.71 us (4%)
    ppermute x3, starting transfers between devices, from_behind(): lax.ppermute(block, CTX, [(i - distance, i) for i in range(distance, coun...  22 us
    all_to_all x1, blocking collectives, round_ring(): lax.all_to_all(sent, CTX + HEAD, 0, 0, tiled=True, axis_index_groups=ring...  15.8 us
    ppermute x1, starting transfers between devices, on_device(): other = lax.ppermute(mine, 'zh', [(0, 1), (1, 0)])  13.9 us
    ppermute x3, waiting for transfers between devices, from_behind(): lax.ppermute(block, CTX, [(i - distance, i) for i in range(distance, coun...  12.9 us
    ppermute x1, waiting for transfers between devices, on_device(): other = lax.ppermute(mine, 'zh', [(0, 1), (1, 0)])  11.8 us
    ppermute x3, starting transfers between devices, along_ring(): return lax.ppermute(block, CTX + HEAD, pairs)  9.82 us
    all_to_all x1, waiting for transfers between devices, round_ring(): lax.all_to_all(sent, CTX + HEAD, 0, 0, tiled=True, axis_index_groups=ring...  6.62 us
    pallas_call x2, Pallas kernels, projection(): pl.pallas_call(body, out_shape=[jax.ShapeDtypeStruct((size, columns), jnp...  6.36 us
  transfers between devices with their start and end apart: 8, of which 3 were waited for; matrix products, arithmetic and copies ran while one was open for 3% of the time, Pallas kernels for 5%

profile of v5, /device:TPU:74, one launch (start us, length us, event | category | flops | bytes accessed | tf_op | source)
XLA Modules:
  0.0 120.1 jit_solution(2861766557322964927)
XLA Ops:
  0.0 1.6 %side_by_side.1 = bf16[168,512]{1,0:T(8,128)(2,1)} custom-call(bf16[168,128]{1,0:T(8,128)(2,1)} %refs_0_.1, bf16[168,128]{1,0:T(8,128)(2,1)} %refs_1_.1, bf16[168,256]{1,0:T(8,128)(2,1)} %refs_2_.1), custom_call_target="tpu_custom_call" | custom-call | tf_op jit(solution)/shard_map/side_by_side/pallas_call | solution.py:70
  1.6 13.9 %collective-permute-start = (bf16[168,512]{1,0:T(8,128)(2,1)}, bf16[168,512]{1,0:T(8,128)(2,1)S(1)}, u32[]{:S(2)}, u32[]{:S(2)}) collective-permute-start(bf16[168,512]{1,0:T(8,128)(2,1)} %side_by_side.1), channel_id=1, source_target_pairs={{0,16},{16,0},{1,17},{17,1},{2,18},{18,2},{3,19},{19,3},{4,20},{20... | collective-permute-start | bytes 516104 | tf_op jit(solution)/shard_map/ppermute | solution.py:200
  15.6 11.8 %collective-permute-done = bf16[168,512]{1,0:T(8,128)(2,1)S(1)} collective-permute-done((bf16[168,512]{1,0:T(8,128)(2,1)}, bf16[168,512]{1,0:T(8,128)(2,1)S(1)}, u32[]{:S(2)}, u32[]{:S(2)}) %collective-permute-start) | collective-permute-done | bytes 172064 | tf_op jit(solution)/shard_map/ppermute | solution.py:200
  27.3 1.1 maximum_select_fusion
  28.4 0.1 broadcast_in_dim.24
  28.6 15.8 %all_to_all.10 = bf16[4,336,512]{2,1,0:T(8,128)(2,1)S(1)} all-to-all(bf16[4,336,512]{2,1,0:T(8,128)(2,1)S(1)} %broadcast_in_dim.24), channel_id=1, replica_groups={{0,32,64,96},{128,160,192,224},{256,288,320,352},{384,416,448,480},{1,1..., dimensions={0} | all-to-all | bytes 2752512 | tf_op jit(solution)/shard_map/all_to_all | solution.py:35
  44.4 1.3 %fusion.6 = (bf16[4,336,256]{2,1,0:T(8,128)(2,1)S(1)}, bf16[1,4,336,256]{3,2,1,0:T(8,128)(2,1)}, bf16[4,336,256]{2,1,0:T(8,128)(2,1)}) fusion(bf16[4,336,512]{2,1,0:T(8,128)(2,1)S(1)} %all_to_all.10), kind=kLoop, calls=%fused_computation.23 | loop fusion | bytes 3440640 | tf_op jit(solution)/shard_map/slice | solution.py:205
  45.6 1.7 %broadcast_in_dim.25 = bf16[4,4,336,256]{3,2,1,0:T(8,128)(2,1)} broadcast(bf16[4,336,256]{2,1,0:T(8,128)(2,1)S(1)} %get-tuple-element.13), dimensions={1,2,3} | broadcast | bytes 3440640 | tf_op jit(solution)/shard_map/broadcast_in_dim | solution.py:34
  47.4 4.9 %all-to-all-start.1 = ((bf16[4,4,336,256]{3,2,1,0:T(8,128)(2,1)}), bf16[4,4,336,256]{3,2,1,0:T(8,128)(2,1)S(1)}, u32[]{:S(2)}, u32[]{:S(2)}) async-start(bf16[4,4,336,256]{3,2,1,0:T(8,128)(2,1)} %broadcast_in_dim.25), calls=%async_computation.1 | async-start | bytes 5505024 | tf_op jit(solution)/shard_map/all_to_all | solution.py:35
  52.3 0.0 copy-start.1
  52.3 0.1 sub.11
  52.4 0.1 mul.51
  52.4 0.1 select_n.52
  52.6 3.4 %collective-permute-start.1 = (bf16[4,336,256]{2,1,0:T(8,128)(2,1)}, bf16[4,336,256]{2,1,0:T(8,128)(2,1)}, u32[]{:S(2)}, u32[]{:S(2)}) collective-permute-start(bf16[4,336,256]{2,1,0:T(8,128)(2,1)} %get-tuple-element.15), channel_id=1, source_target_pairs={{384,0},{0,128},{128,256},{256,384},{416,32},{32,160},{160,288},{2... | collective-permute-start | bytes 2064392 | tf_op jit(solution)/shard_map/ppermute | solution.py:40
  55.9 2.5 %collective-permute-start.2 = (bf16[4,336,256]{2,1,0:T(8,128)(2,1)}, bf16[4,336,256]{2,1,0:T(8,128)(2,1)}, u32[]{:S(2)}, u32[]{:S(2)}) collective-permute-start(bf16[4,336,256]{2,1,0:T(8,128)(2,1)} %get-tuple-element.15), channel_id=1, source_target_pairs={{128,0},{256,128},{384,256},{0,384},{160,32},{288,160},{416,288},{... | collective-permute-start | bytes 2064392 | tf_op jit(solution)/shard_map/ppermute | solution.py:40
  58.4 4.0 %collective-permute-start.3 = (bf16[4,336,256]{2,1,0:T(8,128)(2,1)}, bf16[4,336,256]{2,1,0:T(8,128)(2,1)}, u32[]{:S(2)}, u32[]{:S(2)}) collective-permute-start(bf16[4,336,256]{2,1,0:T(8,128)(2,1)} %get-tuple-element.15), channel_id=1, source_target_pairs={{256,0},{384,128},{0,256},{128,384},{288,32},{416,160},{32,288},{1... | collective-permute-start | bytes 2064392 | tf_op jit(solution)/shard_map/ppermute | solution.py:40
  62.4 0.9 multiply_cosine_fusion
  63.3 0.0 slice-start
  63.3 0.2 maximum_bitcast_fusion
  63.5 0.8 pad_maximum_fusion.1.tables_ref
  64.3 6.6 %all-to-all-done.1 = bf16[4,4,336,256]{3,2,1,0:T(8,128)(2,1)S(1)} async-done(((bf16[4,4,336,256]{3,2,1,0:T(8,128)(2,1)}), bf16[4,4,336,256]{3,2,1,0:T(8,128)(2,1)S(1)}, u32[]{:S(2)}, u32[]{:S(2)}) %all-to-all-start.1) | async-done | bytes 2752544 | tf_op jit(solution)/shard_map/all_to_all | solution.py:35
  70.9 0.0 copy-done.1
  70.9 0.0 copy-start
  70.9 2.4 %copy-done = bf16[448,5376]{1,0:T(8,128)(2,1)S(1)} copy-done((bf16[448,5376]{1,0:T(8,128)(2,1)S(1)}, bf16[448,5376]{1,0:T(8,128)(2,1)}, u32[]{:S(2)}) %copy-start) | copy-done | bytes 4816920
  73.3 0.0 copy-start.3
  73.3 0.0 slice-start.1
  73.3 3.1 %projection.3 = (bf16[448,256]{1,0:T(8,128)(2,1)S(1)}, bf16[128,256]{1,0:T(8,128)(2,1)S(1)}) custom-call(s32[16]{0:T(128)S(1)} %get-tuple-element.19.order_ref, bf16[448,5376]{1,0:T(8,128)(2,1)S(1)} %copy-done, bf16[16,336,256]{2,1,0:T(8,128)(2,1)S(1)} %bitcast.16, f32[1,128]{1,0:T(1,128)S(1)} %bitcast.18, f32[2,448,128]{2,1,0:T(8,128)} %pad_maximum_fusion.1.tables_ref), custom_call_target="tpu_custom_call" | custom-call | tf_op jit(solution)/shard_map/projection/pallas_call | solution.py:112
  76.4 15.5 %collective-permute-start.5 = (bf16[448,256]{1,0:T(8,128)(2,1)S(1)}, bf16[448,256]{1,0:T(8,128)(2,1)S(1)}, u32[]{:S(2)}, u32[]{:S(2)}) collective-permute-start(bf16[448,256]{1,0:T(8,128)(2,1)S(1)} %get-tuple-element.12.refs_3_), channel_id=1, source_target_pairs={{0,16},{16,32},{32,48},{48,64},{64,80},{80,96},{96,112},{112,128},... | collective-permute-start | bytes 688136 | tf_op jit(solution)/shard_map/ppermute | solution.py:45
  91.9 2.3 %collective-permute-start.6 = (bf16[448,256]{1,0:T(8,128)(2,1)S(1)}, bf16[448,256]{1,0:T(8,128)(2,1)S(1)}, u32[]{:S(2)}, u32[]{:S(2)}) collective-permute-start(bf16[448,256]{1,0:T(8,128)(2,1)S(1)} %get-tuple-element.12.refs_3_), channel_id=1, source_target_pairs={{0,32},{16,48},{32,64},{48,80},{64,96},{80,112},{96,128},{112,144}... | collective-permute-start | bytes 688136 | tf_op jit(solution)/shard_map/ppermute | solution.py:45
  94.2 0.0 collective-permute-done.1
  94.2 4.3 %collective-permute-start.4 = (bf16[128,256]{1,0:T(8,128)(2,1)S(1)}, bf16[128,256]{1,0:T(8,128)(2,1)S(1)}, u32[]{:S(2)}, u32[]{:S(2)}) collective-permute-start(bf16[128,256]{1,0:T(8,128)(2,1)S(1)} %get-tuple-element.11), channel_id=1, source_target_pairs={{0,48},{16,64},{32,80},{48,96},{64,112},{80,128},{96,144},{112,160... | collective-permute-start | bytes 196616 | tf_op jit(solution)/shard_map/ppermute | solution.py:45
  98.5 0.0 collective-permute-done.2
  98.5 0.0 collective-permute-done.3
  98.5 0.0 copy-done.3
  98.5 0.0 copy-start.2
  98.5 1.7 %pad_maximum_fusion = bf16[4,4,336,256]{3,2,1,0:T(8,128)(2,1)S(1)} fusion(bf16[1,4,336,256]{3,2,1,0:T(8,128)(2,1)} %bitcast.4, bf16[1,4,336,256]{3,2,1,0:T(8,128)(2,1)} %bitcast.3, bf16[1,4,336,256]{3,2,1,0:T(8,128)(2,1)} %bitcast.2, bf16[1,4,336,256]{3,2,1,0:T(8,128)(2,1)S(1)} %copy-done.3), kind=kLoop, calls=%fused_computation | loop fusion | flops 4128768 | bytes 5505024 | tf_op jit(solution)/shard_map/stack | solution.py:213
  100.2 0.0 slice-done
  100.2 0.0 slice-done.1
  100.2 0.0 copy-done.2
  100.3 3.3 %projection.2.queries_ref = bf16[448,256]{1,0:T(8,128)(2,1)S(1)} custom-call(s32[16]{0:T(128)S(1)} %get-tuple-element.20.order_ref, bf16[448,5376]{1,0:T(8,128)(2,1)S(1)} %bitcast.15, bf16[16,336,256]{2,1,0:T(8,128)(2,1)S(1)} %bitcast.17, f32[1,128]{1,0:T(1,128)S(1)} %bitcast.19, f32[2,448,128]{2,1,0:T(8,128)} %pad_maximum_fusion.1.tables_ref), custom_call_target="tpu_custom_call" | custom-call | tf_op jit(solution)/shard_map/projection/pallas_call | solution.py:112
  103.5 12.9 %collective-permute-done.4.refs_0_ = bf16[128,256]{1,0:T(8,128)(2,1)S(1)} collective-permute-done((bf16[128,256]{1,0:T(8,128)(2,1)S(1)}, bf16[128,256]{1,0:T(8,128)(2,1)S(1)}, u32[]{:S(2)}, u32[]{:S(2)}) %collective-permute-start.4) | collective-permute-done | bytes 65568 | tf_op jit(solution)/shard_map/ppermute | solution.py:45
  116.5 0.0 collective-permute-done.5.refs_1_
  116.5 0.0 collective-permute-done.6.refs_2_
  116.5 3.6 %attention.1 = bf16[448,256]{1,0:T(8,128)(2,1)} custom-call(s32[1]{0:T(128)} %bitcast.offset_ref, bf16[448,256]{1,0:T(8,128)(2,1)S(1)} %projection.2.queries_ref, bf16[128,256]{1,0:T(8,128)(2,1)S(1)} %collective-permute-done.4.refs_0_, bf16[448,256]{1,0:T(8,128)(2,1)S(1)} %collective-permute-done.5.refs_1_, ...), custom_call_target="tpu_custom_call" | custom-call | flops 499122176 | bytes 1212416 | tf_op jit(solution)/shard_map/attention/pallas_call | solution.py:177
  (6 shorter events, 0.0 us)
Async XLA Ops:
  1.6 25.7 %collective-permute-start = (bf16[168,512]{1,0:T(8,128)(2,1)}, bf16[168,512]{1,0:T(8,128)(2,1)S(1)}, u32[]{:S(2)}, u32[]{:S(2)}) collective-permute-start(bf16[168,512]{1,0:T(8,128)(2,1)} %side_by_side.1), channel_id=1, source_target_pairs={{0,16},{16,0},{1,17},{17,1},{2,18},{18,2},{3,19},{19,3},{4,20},{20... | collective-permute-start | bytes 516104 | tf_op jit(solution)/shard_map/ppermute | solution.py:200
  47.4 23.6 %all-to-all-start.1 = ((bf16[4,4,336,256]{3,2,1,0:T(8,128)(2,1)}), bf16[4,4,336,256]{3,2,1,0:T(8,128)(2,1)S(1)}, u32[]{:S(2)}, u32[]{:S(2)}) async-start(bf16[4,4,336,256]{3,2,1,0:T(8,128)(2,1)} %broadcast_in_dim.25), calls=%async_computation.1 | async-start | bytes 5505024 | tf_op jit(solution)/shard_map/all_to_all | solution.py:35
  52.3 18.7 %copy-start.1 = (f32[128]{0:T(128)S(1)}, f32[128]{0:T(128)}, u32[]{:S(2)}) copy-start(f32[128]{0:T(128)} %param.11) | copy-start | bytes 1540
  52.6 41.7 %collective-permute-start.1 = (bf16[4,336,256]{2,1,0:T(8,128)(2,1)}, bf16[4,336,256]{2,1,0:T(8,128)(2,1)}, u32[]{:S(2)}, u32[]{:S(2)}) collective-permute-start(bf16[4,336,256]{2,1,0:T(8,128)(2,1)} %get-tuple-element.15), channel_id=1, source_target_pairs={{384,0},{0,128},{128,256},{256,384},{416,32},{32,160},{160,288},{2... | collective-permute-start | bytes 2064392 | tf_op jit(solution)/shard_map/ppermute | solution.py:40
  55.9 42.5 %collective-permute-start.2 = (bf16[4,336,256]{2,1,0:T(8,128)(2,1)}, bf16[4,336,256]{2,1,0:T(8,128)(2,1)}, u32[]{:S(2)}, u32[]{:S(2)}) collective-permute-start(bf16[4,336,256]{2,1,0:T(8,128)(2,1)} %get-tuple-element.15), channel_id=1, source_target_pairs={{128,0},{256,128},{384,256},{0,384},{160,32},{288,160},{416,288},{... | collective-permute-start | bytes 2064392 | tf_op jit(solution)/shard_map/ppermute | solution.py:40
  58.4 40.1 %collective-permute-start.3 = (bf16[4,336,256]{2,1,0:T(8,128)(2,1)}, bf16[4,336,256]{2,1,0:T(8,128)(2,1)}, u32[]{:S(2)}, u32[]{:S(2)}) collective-permute-start(bf16[4,336,256]{2,1,0:T(8,128)(2,1)} %get-tuple-element.15), channel_id=1, source_target_pairs={{256,0},{384,128},{0,256},{128,384},{288,32},{416,160},{32,288},{1... | collective-permute-start | bytes 2064392 | tf_op jit(solution)/shard_map/ppermute | solution.py:40
  63.3 36.9 %slice-start = ((s8[4816896]{0:T(1024)(128)(4,1)}), s8[622592]{0:T(1024)(128)(4,1)S(1)}, s32[]{:S(2)}) async-start(s8[4816896]{0:T(1024)(128)(4,1)} %bitcast.14), calls=%async_computation.2 | async-start | bytes 1245184
  70.9 2.4 %copy-start = (bf16[448,5376]{1,0:T(8,128)(2,1)S(1)}, bf16[448,5376]{1,0:T(8,128)(2,1)}, u32[]{:S(2)}) copy-start(bf16[448,5376]{1,0:T(8,128)(2,1)} %tokens_ref.3) | copy-start | bytes 14450692
  73.3 25.2 %copy-start.3 = (bf16[1,4,336,256]{3,2,1,0:T(8,128)(2,1)S(1)}, bf16[1,4,336,256]{3,2,1,0:T(8,128)(2,1)}, u32[]{:S(2)}) copy-start(bf16[1,4,336,256]{3,2,1,0:T(8,128)(2,1)} %get-tuple-element.14) | copy-start | bytes 2064388
  73.3 26.9 %slice-start.1 = ((s8[4816896]{0:T(1024)(128)(4,1)}), s8[4194304]{0:T(1024)(128)(4,1)S(1)}, s32[]{:S(2)}) async-start(s8[4816896]{0:T(1024)(128)(4,1)} %bitcast.14), calls=%async_computation.3 | async-start | bytes 8388608
  76.4 40.0 %collective-permute-start.5 = (bf16[448,256]{1,0:T(8,128)(2,1)S(1)}, bf16[448,256]{1,0:T(8,128)(2,1)S(1)}, u32[]{:S(2)}, u32[]{:S(2)}) collective-permute-start(bf16[448,256]{1,0:T(8,128)(2,1)S(1)} %get-tuple-element.12.refs_3_), channel_id=1, source_target_pairs={{0,16},{16,32},{32,48},{48,64},{64,80},{80,96},{96,112},{112,128},... | collective-permute-start | bytes 688136 | tf_op jit(solution)/shard_map/ppermute | solution.py:45
  91.9 24.6 %collective-permute-start.6 = (bf16[448,256]{1,0:T(8,128)(2,1)S(1)}, bf16[448,256]{1,0:T(8,128)(2,1)S(1)}, u32[]{:S(2)}, u32[]{:S(2)}) collective-permute-start(bf16[448,256]{1,0:T(8,128)(2,1)S(1)} %get-tuple-element.12.refs_3_), channel_id=1, source_target_pairs={{0,32},{16,48},{32,64},{48,80},{64,96},{80,112},{96,128},{112,144}... | collective-permute-start | bytes 688136 | tf_op jit(solution)/shard_map/ppermute | solution.py:45
  94.2 22.2 %collective-permute-start.4 = (bf16[128,256]{1,0:T(8,128)(2,1)S(1)}, bf16[128,256]{1,0:T(8,128)(2,1)S(1)}, u32[]{:S(2)}, u32[]{:S(2)}) collective-permute-start(bf16[128,256]{1,0:T(8,128)(2,1)S(1)} %get-tuple-element.11), channel_id=1, source_target_pairs={{0,48},{16,64},{32,80},{48,96},{64,112},{80,128},{96,144},{112,160... | collective-permute-start | bytes 196616 | tf_op jit(solution)/shard_map/ppermute | solution.py:45
  98.5 1.7 %copy-start.2 = (f32[128]{0:T(128)S(1)}, f32[128]{0:T(128)}, u32[]{:S(2)}) copy-start(f32[128]{0:T(128)} %param.10) | copy-start | bytes 1540

commit v6 on v4

--- a/solution.py
+++ b/solution.py
@@ -13,7 +13,7 @@
 SHIFTS = (0, 1, 3, 2)
 CTX = ("y", "x", "zh")
 HEAD = ("zl", "core")
-QUERY_BLOCK = 64
+QUERY_BLOCK = 112
 OPERANDS = (0, 2, 1, 3)
 
 query_scale = 168.0 ** (-0.5)

time: 121 us -> 120 us (level)
  no operation moved by 1% of the time
where the time goes in v6:
time: 120 us
  starting transfers between devices  50.7 us (42%)
  waiting for transfers between devices  31.3 us (26%)
  blocking collectives  15.8 us (13%)
  Pallas kernels  11 us (9%)
  local copies, waits for them, and re-layouts  5.73 us (5%)
  other arithmetic  4.71 us (4%)
    ppermute x3, starting transfers between devices, from_behind(): lax.ppermute(block, CTX, [(i - distance, i) for i in range(distance, coun...  22 us
    all_to_all x1, blocking collectives, round_ring(): lax.all_to_all(sent, CTX + HEAD, 0, 0, tiled=True, axis_index_groups=ring...  15.8 us
    ppermute x1, starting transfers between devices, on_device(): other = lax.ppermute(mine, 'zh', [(0, 1), (1, 0)])  13.9 us
    ppermute x3, waiting for transfers between devices, from_behind(): lax.ppermute(block, CTX, [(i - distance, i) for i in range(distance, coun...  12.9 us
    ppermute x1, waiting for transfers between devices, on_device(): other = lax.ppermute(mine, 'zh', [(0, 1), (1, 0)])  11.8 us
    ppermute x3, starting transfers between devices, along_ring(): return lax.ppermute(block, CTX + HEAD, pairs)  9.82 us
    all_to_all x1, waiting for transfers between devices, round_ring(): lax.all_to_all(sent, CTX + HEAD, 0, 0, tiled=True, axis_index_groups=ring...  6.62 us
    pallas_call x2, Pallas kernels, projection(): pl.pallas_call(body, out_shape=[jax.ShapeDtypeStruct((size, columns), jnp...  6.36 us
  transfers between devices with their start and end apart: 8, of which 3 were waited for; matrix products, arithmetic and copies ran while one was open for 3% of the time, Pallas kernels for 5%

profile of v6, /device:TPU:74, one launch (start us, length us, event | category | flops | bytes accessed | tf_op | source)
XLA Modules:
  0.0 119.5 jit_solution(14252534660600729819)
XLA Ops:
  0.0 1.6 %side_by_side.1 = bf16[168,512]{1,0:T(8,128)(2,1)} custom-call(bf16[168,128]{1,0:T(8,128)(2,1)} %refs_0_.1, bf16[168,128]{1,0:T(8,128)(2,1)} %refs_1_.1, bf16[168,256]{1,0:T(8,128)(2,1)} %refs_2_.1), custom_call_target="tpu_custom_call" | custom-call | tf_op jit(solution)/shard_map/side_by_side/pallas_call | solution.py:68
  1.6 13.9 %collective-permute-start = (bf16[168,512]{1,0:T(8,128)(2,1)}, bf16[168,512]{1,0:T(8,128)(2,1)S(1)}, u32[]{:S(2)}, u32[]{:S(2)}) collective-permute-start(bf16[168,512]{1,0:T(8,128)(2,1)} %side_by_side.1), channel_id=1, source_target_pairs={{0,16},{16,0},{1,17},{17,1},{2,18},{18,2},{3,19},{19,3},{4,20},{20... | collective-permute-start | bytes 516104 | tf_op jit(solution)/shard_map/ppermute | solution.py:198
  15.6 11.8 %collective-permute-done = bf16[168,512]{1,0:T(8,128)(2,1)S(1)} collective-permute-done((bf16[168,512]{1,0:T(8,128)(2,1)}, bf16[168,512]{1,0:T(8,128)(2,1)S(1)}, u32[]{:S(2)}, u32[]{:S(2)}) %collective-permute-start) | collective-permute-done | bytes 172064 | tf_op jit(solution)/shard_map/ppermute | solution.py:198
  27.3 1.1 maximum_select_fusion
  28.4 0.1 broadcast_in_dim.24
  28.6 15.8 %all_to_all.10 = bf16[4,336,512]{2,1,0:T(8,128)(2,1)S(1)} all-to-all(bf16[4,336,512]{2,1,0:T(8,128)(2,1)S(1)} %broadcast_in_dim.24), channel_id=1, replica_groups={{0,32,64,96},{128,160,192,224},{256,288,320,352},{384,416,448,480},{1,1..., dimensions={0} | all-to-all | bytes 2752512 | tf_op jit(solution)/shard_map/all_to_all | solution.py:33
  44.4 1.3 %fusion.6 = (bf16[4,336,256]{2,1,0:T(8,128)(2,1)S(1)}, bf16[1,4,336,256]{3,2,1,0:T(8,128)(2,1)}, bf16[4,336,256]{2,1,0:T(8,128)(2,1)}) fusion(bf16[4,336,512]{2,1,0:T(8,128)(2,1)S(1)} %all_to_all.10), kind=kLoop, calls=%fused_computation.23 | loop fusion | bytes 3440640 | tf_op jit(solution)/shard_map/slice | solution.py:203
  45.6 1.7 %broadcast_in_dim.25 = bf16[4,4,336,256]{3,2,1,0:T(8,128)(2,1)} broadcast(bf16[4,336,256]{2,1,0:T(8,128)(2,1)S(1)} %get-tuple-element.13), dimensions={1,2,3} | broadcast | bytes 3440640 | tf_op jit(solution)/shard_map/broadcast_in_dim | solution.py:32
  47.4 4.9 %all-to-all-start.1 = ((bf16[4,4,336,256]{3,2,1,0:T(8,128)(2,1)}), bf16[4,4,336,256]{3,2,1,0:T(8,128)(2,1)S(1)}, u32[]{:S(2)}, u32[]{:S(2)}) async-start(bf16[4,4,336,256]{3,2,1,0:T(8,128)(2,1)} %broadcast_in_dim.25), calls=%async_computation.1 | async-start | bytes 5505024 | tf_op jit(solution)/shard_map/all_to_all | solution.py:33
  52.3 0.0 copy-start.1
  52.3 0.1 sub.11
  52.4 0.1 mul.51
  52.4 0.1 select_n.52
  52.6 3.4 %collective-permute-start.1 = (bf16[4,336,256]{2,1,0:T(8,128)(2,1)}, bf16[4,336,256]{2,1,0:T(8,128)(2,1)}, u32[]{:S(2)}, u32[]{:S(2)}) collective-permute-start(bf16[4,336,256]{2,1,0:T(8,128)(2,1)} %get-tuple-element.15), channel_id=1, source_target_pairs={{384,0},{0,128},{128,256},{256,384},{416,32},{32,160},{160,288},{2... | collective-permute-start | bytes 2064392 | tf_op jit(solution)/shard_map/ppermute | solution.py:38
  55.9 2.5 %collective-permute-start.2 = (bf16[4,336,256]{2,1,0:T(8,128)(2,1)}, bf16[4,336,256]{2,1,0:T(8,128)(2,1)}, u32[]{:S(2)}, u32[]{:S(2)}) collective-permute-start(bf16[4,336,256]{2,1,0:T(8,128)(2,1)} %get-tuple-element.15), channel_id=1, source_target_pairs={{128,0},{256,128},{384,256},{0,384},{160,32},{288,160},{416,288},{... | collective-permute-start | bytes 2064392 | tf_op jit(solution)/shard_map/ppermute | solution.py:38
  58.4 4.0 %collective-permute-start.3 = (bf16[4,336,256]{2,1,0:T(8,128)(2,1)}, bf16[4,336,256]{2,1,0:T(8,128)(2,1)}, u32[]{:S(2)}, u32[]{:S(2)}) collective-permute-start(bf16[4,336,256]{2,1,0:T(8,128)(2,1)} %get-tuple-element.15), channel_id=1, source_target_pairs={{256,0},{384,128},{0,256},{128,384},{288,32},{416,160},{32,288},{1... | collective-permute-start | bytes 2064392 | tf_op jit(solution)/shard_map/ppermute | solution.py:38
  62.4 0.9 multiply_cosine_fusion
  63.3 0.0 slice-start
  63.3 0.2 maximum_bitcast_fusion
  63.5 0.8 pad_maximum_fusion.1.tables_ref
  64.3 6.6 %all-to-all-done.1 = bf16[4,4,336,256]{3,2,1,0:T(8,128)(2,1)S(1)} async-done(((bf16[4,4,336,256]{3,2,1,0:T(8,128)(2,1)}), bf16[4,4,336,256]{3,2,1,0:T(8,128)(2,1)S(1)}, u32[]{:S(2)}, u32[]{:S(2)}) %all-to-all-start.1) | async-done | bytes 2752544 | tf_op jit(solution)/shard_map/all_to_all | solution.py:33
  70.9 0.0 copy-done.1
  70.9 0.0 copy-start
  70.9 2.4 %copy-done = bf16[448,5376]{1,0:T(8,128)(2,1)S(1)} copy-done((bf16[448,5376]{1,0:T(8,128)(2,1)S(1)}, bf16[448,5376]{1,0:T(8,128)(2,1)}, u32[]{:S(2)}) %copy-start) | copy-done | bytes 4816920
  73.3 0.0 copy-start.3
  73.3 0.0 slice-start.1
  73.3 3.1 %projection.3 = (bf16[448,256]{1,0:T(8,128)(2,1)S(1)}, bf16[128,256]{1,0:T(8,128)(2,1)S(1)}) custom-call(s32[16]{0:T(128)S(1)} %get-tuple-element.19.order_ref, bf16[448,5376]{1,0:T(8,128)(2,1)S(1)} %copy-done, bf16[16,336,256]{2,1,0:T(8,128)(2,1)S(1)} %bitcast.16, f32[1,128]{1,0:T(1,128)S(1)} %bitcast.18, f32[2,448,128]{2,1,0:T(8,128)} %pad_maximum_fusion.1.tables_ref), custom_call_target="tpu_custom_call" | custom-call | tf_op jit(solution)/shard_map/projection/pallas_call | solution.py:110
  76.4 15.5 %collective-permute-start.5 = (bf16[448,256]{1,0:T(8,128)(2,1)S(1)}, bf16[448,256]{1,0:T(8,128)(2,1)S(1)}, u32[]{:S(2)}, u32[]{:S(2)}) collective-permute-start(bf16[448,256]{1,0:T(8,128)(2,1)S(1)} %get-tuple-element.12.refs_3_), channel_id=1, source_target_pairs={{0,16},{16,32},{32,48},{48,64},{64,80},{80,96},{96,112},{112,128},... | collective-permute-start | bytes 688136 | tf_op jit(solution)/shard_map/ppermute | solution.py:43
  91.9 2.3 %collective-permute-start.6 = (bf16[448,256]{1,0:T(8,128)(2,1)S(1)}, bf16[448,256]{1,0:T(8,128)(2,1)S(1)}, u32[]{:S(2)}, u32[]{:S(2)}) collective-permute-start(bf16[448,256]{1,0:T(8,128)(2,1)S(1)} %get-tuple-element.12.refs_3_), channel_id=1, source_target_pairs={{0,32},{16,48},{32,64},{48,80},{64,96},{80,112},{96,128},{112,144}... | collective-permute-start | bytes 688136 | tf_op jit(solution)/shard_map/ppermute | solution.py:43
  94.2 0.0 collective-permute-done.1
  94.2 4.3 %collective-permute-start.4 = (bf16[128,256]{1,0:T(8,128)(2,1)S(1)}, bf16[128,256]{1,0:T(8,128)(2,1)S(1)}, u32[]{:S(2)}, u32[]{:S(2)}) collective-permute-start(bf16[128,256]{1,0:T(8,128)(2,1)S(1)} %get-tuple-element.11), channel_id=1, source_target_pairs={{0,48},{16,64},{32,80},{48,96},{64,112},{80,128},{96,144},{112,160... | collective-permute-start | bytes 196616 | tf_op jit(solution)/shard_map/ppermute | solution.py:43
  98.5 0.0 collective-permute-done.2
  98.5 0.0 collective-permute-done.3
  98.5 0.0 copy-done.3
  98.5 0.0 copy-start.2
  98.5 1.7 %pad_maximum_fusion = bf16[4,4,336,256]{3,2,1,0:T(8,128)(2,1)S(1)} fusion(bf16[1,4,336,256]{3,2,1,0:T(8,128)(2,1)} %bitcast.4, bf16[1,4,336,256]{3,2,1,0:T(8,128)(2,1)} %bitcast.3, bf16[1,4,336,256]{3,2,1,0:T(8,128)(2,1)} %bitcast.2, bf16[1,4,336,256]{3,2,1,0:T(8,128)(2,1)S(1)} %copy-done.3), kind=kLoop, calls=%fused_computation | loop fusion | flops 4128768 | bytes 5505024 | tf_op jit(solution)/shard_map/stack | solution.py:211
  100.2 0.0 slice-done
  100.2 0.0 slice-done.1
  100.2 0.0 copy-done.2
  100.3 3.3 %projection.2.queries_ref = bf16[448,256]{1,0:T(8,128)(2,1)S(1)} custom-call(s32[16]{0:T(128)S(1)} %get-tuple-element.20.order_ref, bf16[448,5376]{1,0:T(8,128)(2,1)S(1)} %bitcast.15, bf16[16,336,256]{2,1,0:T(8,128)(2,1)S(1)} %bitcast.17, f32[1,128]{1,0:T(1,128)S(1)} %bitcast.19, f32[2,448,128]{2,1,0:T(8,128)} %pad_maximum_fusion.1.tables_ref), custom_call_target="tpu_custom_call" | custom-call | tf_op jit(solution)/shard_map/projection/pallas_call | solution.py:110
  103.5 12.9 %collective-permute-done.4.refs_0_ = bf16[128,256]{1,0:T(8,128)(2,1)S(1)} collective-permute-done((bf16[128,256]{1,0:T(8,128)(2,1)S(1)}, bf16[128,256]{1,0:T(8,128)(2,1)S(1)}, u32[]{:S(2)}, u32[]{:S(2)}) %collective-permute-start.4) | collective-permute-done | bytes 65568 | tf_op jit(solution)/shard_map/ppermute | solution.py:43
  116.5 0.0 collective-permute-done.5.refs_1_
  116.5 0.0 collective-permute-done.6.refs_2_
  116.5 3.1 %attention.1 = bf16[448,256]{1,0:T(8,128)(2,1)} custom-call(s32[1]{0:T(128)} %bitcast.offset_ref, bf16[448,256]{1,0:T(8,128)(2,1)S(1)} %projection.2.queries_ref, bf16[128,256]{1,0:T(8,128)(2,1)S(1)} %collective-permute-done.4.refs_0_, bf16[448,256]{1,0:T(8,128)(2,1)S(1)} %collective-permute-done.5.refs_1_, ...), custom_call_target="tpu_custom_call" | custom-call | flops 521142272 | bytes 1212416 | tf_op jit(solution)/shard_map/attention/pallas_call | solution.py:175
  (6 shorter events, 0.0 us)
Async XLA Ops:
  1.6 25.7 %collective-permute-start = (bf16[168,512]{1,0:T(8,128)(2,1)}, bf16[168,512]{1,0:T(8,128)(2,1)S(1)}, u32[]{:S(2)}, u32[]{:S(2)}) collective-permute-start(bf16[168,512]{1,0:T(8,128)(2,1)} %side_by_side.1), channel_id=1, source_target_pairs={{0,16},{16,0},{1,17},{17,1},{2,18},{18,2},{3,19},{19,3},{4,20},{20... | collective-permute-start | bytes 516104 | tf_op jit(solution)/shard_map/ppermute | solution.py:198
  47.4 23.6 %all-to-all-start.1 = ((bf16[4,4,336,256]{3,2,1,0:T(8,128)(2,1)}), bf16[4,4,336,256]{3,2,1,0:T(8,128)(2,1)S(1)}, u32[]{:S(2)}, u32[]{:S(2)}) async-start(bf16[4,4,336,256]{3,2,1,0:T(8,128)(2,1)} %broadcast_in_dim.25), calls=%async_computation.1 | async-start | bytes 5505024 | tf_op jit(solution)/shard_map/all_to_all | solution.py:33
  52.3 18.7 %copy-start.1 = (f32[128]{0:T(128)S(1)}, f32[128]{0:T(128)}, u32[]{:S(2)}) copy-start(f32[128]{0:T(128)} %param.11) | copy-start | bytes 1540
  52.6 41.7 %collective-permute-start.1 = (bf16[4,336,256]{2,1,0:T(8,128)(2,1)}, bf16[4,336,256]{2,1,0:T(8,128)(2,1)}, u32[]{:S(2)}, u32[]{:S(2)}) collective-permute-start(bf16[4,336,256]{2,1,0:T(8,128)(2,1)} %get-tuple-element.15), channel_id=1, source_target_pairs={{384,0},{0,128},{128,256},{256,384},{416,32},{32,160},{160,288},{2... | collective-permute-start | bytes 2064392 | tf_op jit(solution)/shard_map/ppermute | solution.py:38
  55.9 42.5 %collective-permute-start.2 = (bf16[4,336,256]{2,1,0:T(8,128)(2,1)}, bf16[4,336,256]{2,1,0:T(8,128)(2,1)}, u32[]{:S(2)}, u32[]{:S(2)}) collective-permute-start(bf16[4,336,256]{2,1,0:T(8,128)(2,1)} %get-tuple-element.15), channel_id=1, source_target_pairs={{128,0},{256,128},{384,256},{0,384},{160,32},{288,160},{416,288},{... | collective-permute-start | bytes 2064392 | tf_op jit(solution)/shard_map/ppermute | solution.py:38
  58.4 40.1 %collective-permute-start.3 = (bf16[4,336,256]{2,1,0:T(8,128)(2,1)}, bf16[4,336,256]{2,1,0:T(8,128)(2,1)}, u32[]{:S(2)}, u32[]{:S(2)}) collective-permute-start(bf16[4,336,256]{2,1,0:T(8,128)(2,1)} %get-tuple-element.15), channel_id=1, source_target_pairs={{256,0},{384,128},{0,256},{128,384},{288,32},{416,160},{32,288},{1... | collective-permute-start | bytes 2064392 | tf_op jit(solution)/shard_map/ppermute | solution.py:38
  63.3 36.9 %slice-start = ((s8[4816896]{0:T(1024)(128)(4,1)}), s8[622592]{0:T(1024)(128)(4,1)S(1)}, s32[]{:S(2)}) async-start(s8[4816896]{0:T(1024)(128)(4,1)} %bitcast.14), calls=%async_computation.2 | async-start | bytes 1245184
  70.9 2.4 %copy-start = (bf16[448,5376]{1,0:T(8,128)(2,1)S(1)}, bf16[448,5376]{1,0:T(8,128)(2,1)}, u32[]{:S(2)}) copy-start(bf16[448,5376]{1,0:T(8,128)(2,1)} %tokens_ref.3) | copy-start | bytes 14450692
  73.3 25.2 %copy-start.3 = (bf16[1,4,336,256]{3,2,1,0:T(8,128)(2,1)S(1)}, bf16[1,4,336,256]{3,2,1,0:T(8,128)(2,1)}, u32[]{:S(2)}) copy-start(bf16[1,4,336,256]{3,2,1,0:T(8,128)(2,1)} %get-tuple-element.14) | copy-start | bytes 2064388
  73.3 26.9 %slice-start.1 = ((s8[4816896]{0:T(1024)(128)(4,1)}), s8[4194304]{0:T(1024)(128)(4,1)S(1)}, s32[]{:S(2)}) async-start(s8[4816896]{0:T(1024)(128)(4,1)} %bitcast.14), calls=%async_computation.3 | async-start | bytes 8388608
  76.4 40.0 %collective-permute-start.5 = (bf16[448,256]{1,0:T(8,128)(2,1)S(1)}, bf16[448,256]{1,0:T(8,128)(2,1)S(1)}, u32[]{:S(2)}, u32[]{:S(2)}) collective-permute-start(bf16[448,256]{1,0:T(8,128)(2,1)S(1)} %get-tuple-element.12.refs_3_), channel_id=1, source_target_pairs={{0,16},{16,32},{32,48},{48,64},{64,80},{80,96},{96,112},{112,128},... | collective-permute-start | bytes 688136 | tf_op jit(solution)/shard_map/ppermute | solution.py:43
  91.9 24.6 %collective-permute-start.6 = (bf16[448,256]{1,0:T(8,128)(2,1)S(1)}, bf16[448,256]{1,0:T(8,128)(2,1)S(1)}, u32[]{:S(2)}, u32[]{:S(2)}) collective-permute-start(bf16[448,256]{1,0:T(8,128)(2,1)S(1)} %get-tuple-element.12.refs_3_), channel_id=1, source_target_pairs={{0,32},{16,48},{32,64},{48,80},{64,96},{80,112},{96,128},{112,144}... | collective-permute-start | bytes 688136 | tf_op jit(solution)/shard_map/ppermute | solution.py:43
  94.2 22.2 %collective-permute-start.4 = (bf16[128,256]{1,0:T(8,128)(2,1)S(1)}, bf16[128,256]{1,0:T(8,128)(2,1)S(1)}, u32[]{:S(2)}, u32[]{:S(2)}) collective-permute-start(bf16[128,256]{1,0:T(8,128)(2,1)S(1)} %get-tuple-element.11), channel_id=1, source_target_pairs={{0,48},{16,64},{32,80},{48,96},{64,112},{80,128},{96,144},{112,160... | collective-permute-start | bytes 196616 | tf_op jit(solution)/shard_map/ppermute | solution.py:43
  98.5 1.7 %copy-start.2 = (f32[128]{0:T(128)S(1)}, f32[128]{0:T(128)}, u32[]{:S(2)}) copy-start(f32[128]{0:T(128)} %param.10) | copy-start | bytes 1540
